TPU v7x, 32 devices: a whole 2x2x4 slice. The times are simulated.
32 devices in a mesh: tm: 4 (over y, x), region: 8 (over z, core).
Axes of the slice: x: 2, y: 2, z: 4, core: 2. Of those that a mesh axis runs over, the one named last changes fastest.
Arguments:
- gen: float32 [8, 128, 4, 128], P('region', None, 'tm'), may hold values from 0 to 1
- flow: float32 [32, 128, 4, 128], P('region', None, 'tm'), may hold values from -4 to 4
- price: float32 [32, 128, 4, 128], P('region', None, 'tm'), may hold values from -6 to 6
- ramp_dual: float32 [8, 128, 4, 128], P('region', None, 'tm'), may hold values from -3 to 3
- demand: float32 [32, 128, 4, 128], P('region', None, 'tm'), may hold values from -6 to 6
- incid_tiles: bfloat16 [256, 128, 128], P('region'), may hold values from -0.1875 to 0.1875
- tile_bus: int32 [256], P('region'), may hold values from 0 to 3
- tile_line: int32 [256], P('region'), may hold values from 0 to 31, as said below
- gen_tiles: bfloat16 [8, 128, 128], P('region'), may hold values from -0.5 to 0.5
- gen_bus: int32 [8], P('region'), may hold values from 0 to 3
- gen_cost: float32 [8, 128], P('region'), may hold values from 0.1 to 1
- gen_cap: float32 [8, 128], P('region'), may hold values from 0.5 to 2
- ramp_cap: float32 [8, 128], P('region'), may hold values from 0.05 to 0.5
- flow_cap: float32 [32, 128], P('region'), may hold values from 0.3 to 1.5
- weight: float32 [], replicated, may hold values from 0.5 to 2
Outputs:
- gen_next: float32 [8, 128, 4, 128], P('region', None, 'tm')
- flow_next: float32 [32, 128, 4, 128], P('region', None, 'tm')
- price_next: float32 [32, 128, 4, 128], P('region', None, 'tm')
- ramp_next: float32 [8, 128, 4, 128], P('region', None, 'tm')
Inputs may be any that keep to these rules, and one draw needn't show every extreme that they name: Tile t belongs to region r = t // 32; its line block lies in region r - 1, r or r + 1 (those that exist), where region q holds line blocks q * 4 to (q + 1) * 4 - 1. No two tiles have the same pair (tile_bus, tile_line) within a region.
All inputs are finite; a program needn't handle non-finite values.
Results may differ from a plain program's by a relative error of at most 0.0006.
The roundings to bfloat16 on the way count: a program that leaves them out, or rounds other values in their place, can miss the bound.
Values may be sent and summed in bfloat16 or wider, within the bound.
A program may use at most 64 MiB of HBM per device.

v0:
```python
import functools

import jax
import jax.numpy as jnp
from jax import lax
from jax.experimental import pallas as pl
from jax.experimental.pallas import tpu as pltpu
from jax.sharding import PartitionSpec as P

MESH = pl.DeviceIdType.MESH
step_scale = 0.4
tiny = 1e-06
f32 = jnp.float32
bf16 = jnp.bfloat16


def remote(src, dst, send_sem, recv_sem, axis, peer):
    return pltpu.make_async_remote_copy(
        src_ref=src,
        dst_ref=dst,
        send_sem=send_sem,
        recv_sem=recv_sem,
        device_id={axis: peer},
        device_id_type=MESH,
    )


def fold(x):
    rows, columns = x.shape
    y = jnp.sum(x.reshape(rows // 8, 8, columns), axis=0)
    out = y[:, :128]
    for at in range(128, columns, 128):
        out = out + y[:, at : at + 128]
    return out


def both_halves(x):
    row = jnp.sum(x, axis=0, keepdims=True)
    return row + pltpu.roll(row, 64, 1)


def writer(*refs):
    n = (len(refs) - 1) // 2
    copies = [pltpu.make_async_copy(refs[i], refs[n + i], refs[-1].at[i]) for i in range(n)]
    for c in copies:
        c.start()
    for c in copies:
        c.wait()


def kernel(
    dims,
    gen_bus, weight, tile_bus, tile_line, tiles, gtiles, price, flow, gen, ramp, demand, cost, gcap, rcap, fcap,
    o_gen, o_flow, o_price, o_ramp,
    tiles_v, a_v, price_v, flow_v, gen_v, ramp_v, demand_v, cost_v, gcap_v, rcap_v, fcap_v,
    pt_v, own_v, price1_v, flow_s, gen_s, dual_s, genlow_v,
    part_send, part_recv, fw_own, fw_in, d_send, d_recv, b_send, b_recv,
    ar_s, ar_r, acc_v, bus_v, line_v, table_v, table_s,
    in_sem, ps_sem, pr_sem, fs_sem, fr_sem, ds_sem, dr_sem, bs_sem, br_sem,
    as_sem, ar_sem, ready, table_sem,
):
    nt, nr, scen, count_p, count_d = dims
    t = lax.axis_index("tm")
    r = lax.axis_index("region")
    n_tiles, blk, _ = tiles.shape
    n_gens = gtiles.shape[0]
    lines, cols = flow.shape
    buses = price.shape[0]
    lb, bb = lines // blk, buses // blk
    width = 3 * lb + n_gens
    nch = part_send.shape[2]
    cw = lines // nch
    gw = n_gens * blk

    barrier = pltpu.get_barrier_semaphore()
    for axis, me, n in (("region", r, nr), ("tm", t, nt)):
        for k in range(1, n):
            pl.semaphore_signal(
                barrier, inc=1, device_id={axis: lax.rem(me + k, n)}, device_id_type=MESH
            )

    loads = [
        pltpu.make_async_copy(src, dst, in_sem.at[i])
        for i, (src, dst) in enumerate(
            (
                (tile_bus, bus_v),
                (tile_line, line_v),
                (price, price_v),
                (tiles, tiles_v.at[pl.ds(0, n_tiles)]),
                (gtiles, tiles_v.at[pl.ds(n_tiles, n_gens)]),
                (ramp, ramp_v),
                (flow, flow_v),
                (gen, gen_v),
                (fcap, fcap_v),
                (cost, cost_v),
                (gcap, gcap_v),
                (rcap, rcap_v),
                (demand, demand_v),
            )
        )
    ]
    for c in loads:
        c.start()

    tiles_v[n_tiles + n_gens] = jnp.zeros((blk, blk), bf16)

    @pl.when(r == 0)
    def _():
        part_recv[:, 1] = jnp.zeros_like(part_recv[:, 1])
        fw_in[:, 0] = jnp.zeros_like(fw_in[:, 0])

    @pl.when(r == nr - 1)
    def _():
        part_recv[:, 0] = jnp.zeros_like(part_recv[:, 0])
        fw_in[:, 1] = jnp.zeros_like(fw_in[:, 1])

    has = (r > 0, r < nr - 1)
    peer = (jnp.maximum(r - 1, 0), jnp.minimum(r + 1, nr - 1))
    t_next, t_prev = lax.rem(t + 1, nt), lax.rem(t + nt - 1, nt)

    def part_copy(it, side, ch):
        return remote(
            part_send.at[it, side, ch], part_recv.at[it, side, ch],
            ps_sem.at[it, side, ch], pr_sem.at[it, side, ch], "region", peer[side],
        )

    def flow_copy(it, side, ch):
        return remote(
            fw_own.at[it, ch], fw_in.at[it, 1 - side, ch],
            fs_sem.at[it, side, ch], fr_sem.at[it, 1 - side, ch], "region", peer[side],
        )

    def dual_copy(it):
        return remote(d_send.at[it], d_recv.at[it], ds_sem.at[it], dr_sem.at[it], "tm", t_prev)

    def bar_copy(it):
        return remote(b_send.at[it], b_recv.at[it], bs_sem.at[it], br_sem.at[it], "tm", t_next)

    side_at = (0, 2 * lines)

    def build(first, count):
        for w in range(first, first + count):
            for b in range(bb):
                a_v[b * blk : (b + 1) * blk, w * blk : (w + 1) * blk] = tiles_v[table_s[0, b * width + w]]

    def pull_out(it, start_hook=None):
        for ch in range(nch):
            for side in (0, 1):
                at = side_at[side] + ch * cw
                part_send[it, side, ch] = jnp.dot(
                    pt_v[...], a_v[:, at : at + cw], preferred_element_type=f32
                )
                if start_hook is not None and ch == 0 and side == 0:
                    start_hook()

                @pl.when(has[side])
                def _():
                    part_copy(it, side, ch).start()

    def pull_own():
        own_v[:, :lines] = jnp.dot(
            pt_v[...], a_v[:, lines : 2 * lines], preferred_element_type=f32
        )
        own_v[:, lines:] = jnp.dot(
            pt_v[...], a_v[:, 3 * lines :], preferred_element_type=f32
        )

    def set_pt(ref):
        for b in range(bb):
            pt_v[:, b * blk : (b + 1) * blk] = ref[b * blk : (b + 1) * blk, :].T.astype(bf16)

    def row(ref, n):
        return jnp.concatenate([ref[i : i + 1, :] for i in range(n)], axis=1) if n > 1 else ref[...]

    def primal(it, sp):
        acc = jnp.zeros((8, 128), f32)
        per = cw // blk
        for ch in range(nch):
            for side in (0, 1):
                @pl.when(has[1 - side])
                def _():
                    part_copy(it, side, ch).wait_recv()

            lo = ch * cw
            total = own_v[:, lo : lo + cw] + part_recv[it, 0, ch] + part_recv[it, 1, ch]
            cap = jnp.concatenate(
                [fcap_v[ch * per + i : ch * per + i + 1, :] for i in range(per)], axis=1
            )
            now = flow_s[it, :, lo : lo + cw]
            new = jnp.minimum(jnp.maximum(now + sp * total, -cap), cap)
            fw_own[it, ch] = (2.0 * new - now).astype(bf16)
            for side in (0, 1):
                @pl.when(has[side])
                def _():
                    flow_copy(it, side, ch).start()
            flow_s[it + 1, :, lo : lo + cw] = new
            if it == 0:
                acc = acc + fold((new - now) ** 2)
        dual_copy(it).wait_recv()
        dual = dual_s[it]
        nxt = d_recv[it]
        later = nxt if cols == scen else jnp.concatenate([dual[scen:], nxt], axis=0)
        gnow = gen_s[it]
        grad = row(cost_v, n_gens) - own_v[:, lines:] + (dual - later)
        gnew = jnp.minimum(jnp.maximum(gnow - sp * grad, 0.0), row(gcap_v, n_gens))
        gbar = 2.0 * gnew - gnow
        b_send[it] = gbar[cols - scen :]
        bar_copy(it).start()
        gen_s[it + 1] = gnew
        genlow_v[...] = gbar.astype(bf16)
        if it == 0:
            acc = acc + fold((gnew - gnow) ** 2)
        return acc, gbar

    nt_dims = (((1,), (1,)), ((), ()))

    def push(it, finish):
        half = buses // 2
        acc_v[...] = lax.dot_general(
            a_v[:, 3 * lines :], genlow_v[...], nt_dims, preferred_element_type=f32
        )
        for ch in range(nch):
            at = lines + ch * cw
            acc_v[...] += lax.dot_general(
                a_v[:, at : at + cw], fw_own[it, ch], nt_dims, preferred_element_type=f32
            )
        for ch in range(nch):
            for side in (0, 1):
                @pl.when(has[side])
                def _():
                    flow_copy(it, 1 - side, ch).wait_recv()
            for side in (0, 1):
                at = side_at[side] + ch * cw
                acc_v[...] += lax.dot_general(
                    a_v[:, at : at + cw], fw_in[it, side, ch], nt_dims, preferred_element_type=f32
                )

    def ramp_step(it, gbar, sd):
        bar_copy(it).wait_recv()
        prev = b_recv[it]
        earlier = prev if cols == scen else jnp.concatenate([prev, gbar[: cols - scen]], axis=0)
        dual = dual_s[it]
        lifted = dual + sd * (gbar - earlier)
        bound = row(rcap_v, n_gens)
        return lifted - sd * jnp.minimum(jnp.maximum(lifted / sd, -bound), bound)

    zero_at = n_tiles + n_gens
    loads[0].wait()
    loads[1].wait()
    slot = bus_v[...] * width + (line_v[...] - (r - 1) * lb)
    down = lax.broadcasted_iota(jnp.int32, (n_tiles, n_tiles), 0)
    across = lax.broadcasted_iota(jnp.int32, (n_tiles, n_tiles), 1)
    upright = jnp.sum(jnp.where(down == across, slot, 0), axis=1, keepdims=True)
    places = lax.broadcasted_iota(jnp.int32, (n_tiles, 128), 1)
    ids = lax.broadcasted_iota(jnp.int32, (n_tiles, 128), 0)
    found = jnp.sum(jnp.where(upright == places, ids - zero_at, 0), axis=0, keepdims=True)
    lane = lax.broadcasted_iota(jnp.int32, (1, 128), 1)
    for g in range(n_gens):
        found = jnp.where(lane == gen_bus[g] * width + 3 * lb + g, n_tiles + g - zero_at, found)
    table_v[...] = jnp.clip(zero_at + found, 0, zero_at)
    to_scalar = pltpu.make_async_copy(table_v, table_s, table_sem.at[0])
    to_scalar.start()

    w1 = jnp.full((1, 1), weight[0], f32)
    loads[2].wait()
    set_pt(price_v)
    loads[3].wait()
    loads[4].wait()
    to_scalar.wait()
    build(0, lb)
    build(2 * lb, lb)
    loads[5].wait()
    dual_s[0] = ramp_v[...].T
    d_send[0] = dual_s[0][:scen]

    def entered():
        pl.semaphore_wait(barrier, nr - 1 + nt - 1)
        for k in range(1, nr):
            pl.semaphore_signal(
                ready, inc=1, device_id={"region": lax.rem(r + k, nr)}, device_id_type=MESH
            )

    pull_out(0, entered)
    dual_copy(0).start()
    build(lb, lb)
    build(3 * lb, n_gens)
    pull_own()
    for c in loads[6:]:
        c.wait()
    for b in range(lb):
        flow_s[0, :, b * blk : (b + 1) * blk] = flow_v[b * blk : (b + 1) * blk, :].T
    gen_s[0] = gen_v[...].T
    sd1 = step_scale * w1
    primal_acc, gbar1 = primal(0, step_scale / w1)
    push(0, None)
    price_one = price_v[...] + sd1 * (demand_v[...] - acc_v[...])
    price1_v[...] = price_one
    dual_acc = fold((price_one - price_v[...]) ** 2)
    dual_one = ramp_step(0, gbar1, sd1)
    dual_s[1] = dual_one
    dual_acc = dual_acc + fold((dual_one - dual_s[0]) ** 2)

    low = lax.broadcasted_iota(jnp.int32, (1, 128), 1) < 64
    ar_s[...] = jnp.where(low, both_halves(primal_acc), both_halves(dual_acc))
    sums = []
    for j in range(nt):
        for k in range(nr):
            if j or k:
                at = j * nr + k
                sums.append(
                    pltpu.make_async_remote_copy(
                        src_ref=ar_s,
                        dst_ref=ar_r.at[at],
                        send_sem=as_sem.at[at],
                        recv_sem=ar_sem.at[at],
                        device_id={"tm": lax.rem(t + j, nt), "region": lax.rem(r + k, nr)},
                        device_id_type=MESH,
                    )
                )
    pl.semaphore_wait(ready, nr - 1)
    for c in sums:
        c.start()
    d_send[1] = dual_one[:scen]
    set_pt(price1_v)
    pull_out(1)
    dual_copy(1).start()
    pull_own()
    for c in sums:
        c.wait_recv()
    summed = ar_s[...]
    for at in range(1, nt * nr):
        summed = summed + ar_r[at]
    primal_mean = jnp.sum(jnp.where(low, summed, 0.0), axis=1, keepdims=True) / count_p
    dual_mean = jnp.sum(jnp.where(low, 0.0, summed), axis=1, keepdims=True) / count_d
    w2 = jnp.sqrt(w1 * jnp.sqrt((dual_mean + tiny) / (primal_mean + tiny)))

    sd2 = step_scale * w2
    _, gbar2 = primal(1, step_scale / w2)
    for b in range(lb):
        o_flow[b * blk : (b + 1) * blk, :] = flow_s[2, :, b * blk : (b + 1) * blk].T
    o_gen[...] = gen_s[2].T
    push(1, None)
    o_price[...] = price1_v[...] + sd2 * (demand_v[...] - acc_v[...])
    o_ramp[...] = ramp_step(1, gbar2, sd2).T

    for it in range(2):
        for ch in range(nch):
            for side in (0, 1):
                @pl.when(has[side])
                def _():
                    part_copy(it, side, ch).wait_send()
                    flow_copy(it, side, ch).wait_send()
        dual_copy(it).wait_send()
        bar_copy(it).wait_send()
    for c in sums:
        c.wait_send()


def shards(
    gen, flow, price, ramp_dual, demand, incid_tiles, tile_bus, tile_line, gen_tiles, gen_bus,
    gen_cost, gen_cap, ramp_cap, flow_cap, weight,
):
    gb, blk, hours, scen = gen.shape
    lb, bb = flow.shape[0], price.shape[0]
    n_tiles = incid_tiles.shape[0]
    cols = hours * scen
    nt, nr = lax.axis_size("tm"), lax.axis_size("region")
    lines, buses, gens = lb * blk, bb * blk, gb * blk
    width = 3 * lb + gb
    nch = 2 if lb % 2 == 0 else 1
    cw = lines // nch

    dims = (
        nt, nr, scen,
        float((gen.size + flow.size) * nt * nr), float((price.size + ramp_dual.size) * nt * nr),
    )
    any_spec = pl.BlockSpec(memory_space=pl.ANY)
    smem_spec = pl.BlockSpec(memory_space=pltpu.SMEM)
    dma = pltpu.SemaphoreType.DMA
    V = pltpu.VMEM
    scratch = [
        V((n_tiles + gb + 1, blk, blk), bf16),
        V((buses, width * blk), bf16),
        V((buses, cols), f32),
        V((lines, cols), f32),
        V((gens, cols), f32),
        V((gens, cols), f32),
        V((buses, cols), f32),
        V((gb, blk), f32),
        V((gb, blk), f32),
        V((gb, blk), f32),
        V((lb, blk), f32),
        V((cols, buses), bf16),
        V((cols, lines + gens), f32),
        V((buses, cols), f32),
        V((3, cols, lines), f32),
        V((3, cols, gens), f32),
        V((2, cols, gens), f32),
        V((cols, gens), bf16),
        V((2, 2, nch, cols, cw), f32),
        V((2, 2, nch, cols, cw), f32),
        V((2, nch, cols, cw), bf16),
        V((2, 2, nch, cols, cw), bf16),
        V((2, scen, gens), f32),
        V((2, scen, gens), f32),
        V((2, scen, gens), f32),
        V((2, scen, gens), f32),
        V((1, 128), f32),
        V((nt * nr, 1, 128), f32),
        V((buses, cols), f32),
        V((1, n_tiles), jnp.int32),
        V((1, n_tiles), jnp.int32),
        V((1, 128), jnp.int32),
        pltpu.SMEM((1, 128), jnp.int32),
        dma((13,)),
        dma((2, 2, nch)),
        dma((2, 2, nch)),
        dma((2, 2, nch)),
        dma((2, 2, nch)),
        dma((2,)),
        dma((2,)),
        dma((2,)),
        dma((2,)),
        dma((nt * nr,)),
        dma((nt * nr,)),
        pltpu.SemaphoreType.REGULAR,
        dma((1,)),
    ]
    vmem_spec = pl.BlockSpec(memory_space=pltpu.VMEM)
    shapes = ((gens, cols), (lines, cols), (buses, cols), (gens, cols))
    outs = pl.pallas_call(
        functools.partial(kernel, dims),
        out_shape=tuple(V(shape, f32) for shape in shapes),
        in_specs=[smem_spec, smem_spec] + [any_spec] * 13,
        out_specs=(vmem_spec,) * 4,
        scratch_shapes=scratch,
        compiler_params=pltpu.CompilerParams(collective_id=0, has_side_effects=True),
    )(
        gen_bus, weight.reshape(1), tile_bus.reshape(1, n_tiles), tile_line.reshape(1, n_tiles), incid_tiles, gen_tiles,
        price.reshape(buses, cols), flow.reshape(lines, cols), gen.reshape(gens, cols),
        ramp_dual.reshape(gens, cols), demand.reshape(buses, cols),
        gen_cost, gen_cap, ramp_cap, flow_cap,
    )
    outs = pl.pallas_call(
        writer,
        out_shape=tuple(jax.ShapeDtypeStruct(shape, f32) for shape in shapes),
        in_specs=[any_spec] * 4,
        out_specs=(any_spec,) * 4,
        scratch_shapes=[dma((4,))],
    )(*(pltpu.with_memory_space_constraint(out, pltpu.VMEM) for out in outs))
    return tuple(
        out.reshape(like.shape) for out, like in zip(outs, (gen, flow, price, ramp_dual))
    )


def solution(mesh):
    field = P("region", None, "tm", None)
    placed = (
        field, field, field, field, field,
        P("region", None, None), P("region"), P("region"), P("region", None, None), P("region"),
        P("region", None), P("region", None), P("region", None), P("region", None), P(),
    )
    return jax.shard_map(
        shards, mesh=mesh, in_specs=placed, out_specs=(field,) * 4, check_vma=False
    )
```

profile of v0, /device:TPU:0, one launch (start us, length us, event | category | flops | bytes accessed | tf_op | source)
XLA Modules:
  0.0 27.6 jit_solution(1890729676615691392)
XLA Ops:
  1.9 24.8 %shard_map.174 = (f32[128,128]{1,0:T(8,128)S(1)}, f32[512,128]{1,0:T(8,128)S(1)}, f32[512,128]{1,0:T(8,128)S(1)}, f32[128,128]{1,0:T(8,128)S(1)}) custom-call(s32[1]{0:T(128)S(6)} %copy.23.gen_bus, f32[1]{0:T(128)} %bitcast.20.weight, s32[1,32]{1,0:T(1,128)} %bitcast.26, s32[1,32]{1,0:T(1,128)} %bitcast.27, bf16[32,128,128]{2,1,0:T(8,128)(2,1)} %tiles.1, ...), custom_call_target="tpu_custom_call" | custom-call | tf_op jit(solution)/shard_map/pallas_call | solution.py:431
  26.8 0.9 %shard_map.175 = (f32[128,128]{1,0:T(8,128)}, f32[512,128]{1,0:T(8,128)}, f32[512,128]{1,0:T(8,128)}, f32[128,128]{1,0:T(8,128)}) custom-call(f32[128,128]{1,0:T(8,128)S(1)} %get-tuple-element.12.refs_0_, f32[512,128]{1,0:T(8,128)S(1)} %get-tuple-element.13.refs_1_, f32[512,128]{1,0:T(8,128)S(1)} %get-tuple-element.14.refs_2_, ...), custom_call_target="tpu_custom_call" | custom-call | tf_op jit(solution)/shard_map/pallas_call | solution.py:444
where the time goes:
time: 27.8 us; the launch traced here: 27.6 us
  Pallas kernels  25.7 us (92%)
  between operations  1.94 us (7%)
    pallas_call x1, Pallas kernels, shards(): pl.pallas_call(functools.partial(kernel, dims), out_shape=tuple((V(shape,...  24.8 us
    pallas_call x1, Pallas kernels, shards(): pl.pallas_call(writer, out_shape=tuple((jax.ShapeDtypeStruct(shape, f32)...  0.86 us

commit v1 on v0

v1 whole, which is shorter than its diff:
```python
import functools

import jax
import jax.numpy as jnp
from jax import lax
from jax.experimental import pallas as pl
from jax.experimental.pallas import tpu as pltpu
from jax.sharding import PartitionSpec as P

MESH = pl.DeviceIdType.MESH
step_scale = 0.4
tiny = 1e-06
f32 = jnp.float32
bf16 = jnp.bfloat16


def remote(src, dst, send_sem, recv_sem, axis, peer):
    return pltpu.make_async_remote_copy(
        src_ref=src,
        dst_ref=dst,
        send_sem=send_sem,
        recv_sem=recv_sem,
        device_id={axis: peer},
        device_id_type=MESH,
    )


def fold(x):
    rows, columns = x.shape
    y = jnp.sum(x.reshape(rows // 8, 8, columns), axis=0)
    out = y[:, :128]
    for at in range(128, columns, 128):
        out = out + y[:, at : at + 128]
    return out


def both_halves(x):
    row = jnp.sum(x, axis=0, keepdims=True)
    return row + pltpu.roll(row, 64, 1)


def writer(*refs):
    n = (len(refs) - 1) // 2
    copies = [pltpu.make_async_copy(refs[i], refs[n + i], refs[-1].at[i]) for i in range(n)]
    for c in copies:
        c.start()
    for c in copies:
        c.wait()


def flip(x, mask):
    bit = 1
    out = x
    while bit <= mask:
        if mask & bit:
            out = out + bit * (1 - 2 * lax.rem(x // bit, 2))
        bit *= 2
    return out


def partners(x, n):
    if n & (n - 1) == 0:
        return [(m, flip(x, m)) for m in range(n - 1, 0, -1)]
    return [(m, lax.rem(x + m, n)) for m in range(1, n)]


FAR, NEAR = 0, 1


def kernel(
    dims,
    gen_bus, weight, tile_bus, tile_line, tiles, gtiles, price, flow, gen, ramp, demand, cost, gcap, rcap, fcap,
    o_gen, o_flow, o_price, o_ramp,
    tiles_v, a_v, price_v, ramp_v, late_v, caps_v, fcap_v,
    pt_v, own_v, price1_v, flow_s, gen_s, dual_s, genlow_v,
    part_send, part_recv, fw_own, fw_in, d_send, d_recv, v_send, v_recv, prev_v,
    ar_s, ar_r, acc_v, change_v, idx_v, table_v, table_s,
    in_sem, ps_sem, pr_sem, fs_sem, fr_sem, tm_sem, ar_sem, ready, table_sem,
):
    nt, nr, scen, count_p, count_d = dims
    t = lax.axis_index("tm")
    r = lax.axis_index("region")
    n_tiles, blk, _ = tiles.shape
    n_gens = gtiles.shape[0]
    lines, cols = flow.shape
    buses = price.shape[0]
    lb, bb = lines // blk, buses // blk
    width = 3 * lb + n_gens
    gens = gen.shape[0]
    nch = part_send.shape[2]
    cw = lines // nch
    n_stages = ready.shape[0]

    odd = lax.rem(r, 2)
    place = (r - 1 + 2 * odd, r + 1 - 2 * odd)
    has = tuple((p >= 0) & (p < nr) for p in place)
    peer = tuple(jnp.clip(p, 0, nr - 1) for p in place)
    count = tuple(jnp.where(h, 1, 0) for h in has)
    first_window = (2 * lb * odd, 2 * lb * (1 - odd), lb)

    barrier = pltpu.get_barrier_semaphore()
    for side in (FAR, NEAR):
        @pl.when(has[side])
        def _():
            pl.semaphore_signal(
                barrier, inc=1, device_id={"region": peer[side]}, device_id_type=MESH
            )
    for k in range(1, nt):
        pl.semaphore_signal(
            barrier, inc=1, device_id={"tm": lax.rem(t + k, nt)}, device_id_type=MESH
        )

    def stage_signal(stage):
        step = 2**stage
        for to in (r - step, r + step):
            @pl.when((to >= 0) & (to < nr))
            def _():
                pl.semaphore_signal(
                    ready.at[stage], inc=1, device_id={"region": jnp.clip(to, 0, nr - 1)},
                    device_id_type=MESH,
                )

    def stage_wait(stage):
        step = 2**stage
        pl.semaphore_wait(
            ready.at[stage], jnp.where(r >= step, 1, 0) + jnp.where(r + step < nr, 1, 0)
        )

    def pass_on(stage):
        if stage < n_stages - 1:
            stage_wait(stage)
            stage_signal(stage + 1)

    def load(i, *pairs):
        copies = [pltpu.make_async_copy(src, dst, in_sem.at[i]) for src, dst in pairs]
        for c in copies:
            c.start()

    def arrived(i, ref):
        pltpu.make_async_copy(ref, ref, in_sem.at[i]).wait()

    load(0, (tile_bus, idx_v.at[0]), (tile_line, idx_v.at[1]))
    all_tiles = tiles_v.at[pl.ds(0, n_tiles + n_gens)]
    load(1, (price, price_v))
    load(2, (ramp, ramp_v))
    load(3, (tiles, tiles_v.at[pl.ds(0, n_tiles)]), (gtiles, tiles_v.at[pl.ds(n_tiles, n_gens)]))
    flow_v = late_v.at[pl.ds(0, lines)]
    demand_v = late_v.at[pl.ds(lines, buses)]
    gen_v = late_v.at[pl.ds(lines + buses, gens)]

    def late_loads():
        load(4, (flow, flow_v), (demand, demand_v), (gen, gen_v))
        load(5, (cost, caps_v.at[0]), (gcap, caps_v.at[1]), (rcap, caps_v.at[2]))
        load(6, (fcap, fcap_v))

    tiles_v[n_tiles + n_gens] = jnp.zeros((blk, blk), bf16)

    for side in (FAR, NEAR):
        @pl.when(jnp.logical_not(has[side]))
        def _():
            part_recv[:, side] = jnp.zeros_like(part_recv[:, side])
            fw_in[:, side] = jnp.zeros_like(fw_in[:, side])

    t_next, t_prev = lax.rem(t + 1, nt), lax.rem(t + nt - 1, nt)

    def far_part(it, ch):
        return remote(
            part_send.at[it, FAR, ch], part_recv.at[it, FAR, ch],
            ps_sem.at[FAR], pr_sem.at[ch], "region", peer[FAR],
        )

    def near_part(it):
        return remote(
            part_send.at[it, NEAR], part_recv.at[it, NEAR],
            ps_sem.at[NEAR], pr_sem.at[nch], "region", peer[NEAR],
        )

    def far_flow(it, ch):
        return remote(
            fw_own.at[it, ch], fw_in.at[it, FAR, ch],
            fs_sem.at[FAR], fr_sem.at[ch], "region", peer[FAR],
        )

    def near_flow(it):
        return remote(
            fw_own.at[it], fw_in.at[it, NEAR],
            fs_sem.at[NEAR], fr_sem.at[nch], "region", peer[NEAR],
        )

    def dual_copy(it):
        return remote(d_send.at[it], d_recv.at[it], tm_sem.at[0], tm_sem.at[2 + it], "tm", t_prev)

    def prev_copy(it):
        parts = pl.ds(0, 2 - it)
        return remote(
            v_send.at[it, parts], v_recv.at[it, parts], tm_sem.at[1], tm_sem.at[4 + it], "tm", t_next
        )

    def sent(it):
        for side in (FAR, NEAR):
            @pl.when(has[side])
            def _():
                ref = part_send.at[it, side]
                pltpu.make_async_copy(ref, ref, ps_sem.at[side]).wait()
                ref = fw_own.at[it]
                pltpu.make_async_copy(ref, ref, fs_sem.at[side]).wait()

    at_near, at_own, at_gens = lines, 2 * lines, 3 * lines

    def build(group):
        n = n_gens if group == 3 else lb
        for i in range(n):
            window = 3 * lb + i if group == 3 else first_window[group] + i
            lo = group * lines + i * blk
            for b in range(bb):
                a_v[b * blk : (b + 1) * blk, lo : lo + blk] = tiles_v[table_s[0, b * width + window]]

    per_dot = 2 if nch % 2 == 0 else 1

    def far_sums(it, ch):
        sums = jnp.dot(
            pt_v[...], a_v[:, ch * cw : (ch + per_dot) * cw], preferred_element_type=f32
        )
        for i in range(per_dot):
            part_send[it, FAR, ch + i] = sums[:, i * cw : (i + 1) * cw]

    def send_far(it, ch):
        @pl.when(has[FAR])
        def _():
            for i in range(per_dot):
                far_part(it, ch + i).start()

    def pull_near(it):
        for ch in range(0, nch, per_dot):
            at = at_near + ch * cw
            sums = jnp.dot(
                pt_v[...], a_v[:, at : at + per_dot * cw], preferred_element_type=f32
            )
            for i in range(per_dot):
                part_send[it, NEAR, ch + i] = sums[:, i * cw : (i + 1) * cw]

        @pl.when(has[NEAR])
        def _():
            near_part(it).start()

    def pull_gens():
        own_v[:, lines:] = jnp.dot(pt_v[...], a_v[:, at_gens:], preferred_element_type=f32)

    def pull_own():
        own_v[:, :lines] = jnp.dot(
            pt_v[...], a_v[:, at_own:at_gens], preferred_element_type=f32
        )

    def set_pt(ref):
        for b in range(bb):
            pt_v[:, b * blk : (b + 1) * blk] = ref[b * blk : (b + 1) * blk, :].astype(bf16).T

    def row(ref, n):
        return jnp.concatenate([ref[i : i + 1, :] for i in range(n)], axis=1) if n > 1 else ref[...]

    def gen_pull(it):
        grad = row(caps_v.at[0], n_gens) - own_v[:, lines:] + dual_s[it]
        own_v[:, lines:] = grad
        v_send[it, 0] = grad[cols - scen :]
        if it == 0:
            v_send[it, 1] = gen_s[it][cols - scen :]
        prev_copy(it).start()

    def clipped(now, sp, grad):
        return jnp.minimum(jnp.maximum(now - sp * grad, 0.0), row(caps_v.at[1], n_gens))

    def gen_step(it, sp):
        dual_copy(it).wait_recv()
        nxt = d_recv[it]
        later = nxt if cols == scen else jnp.concatenate([dual_s[it][scen:], nxt], axis=0)
        gnow = gen_s[it]
        gnew = clipped(gnow, sp, own_v[:, lines:] - later)
        gbar = 2.0 * gnew - gnow
        gen_s[it + 1] = gnew
        genlow_v[...] = gbar.astype(bf16)
        return (gnew - gnow) ** 2, gbar

    def prev_bar(it, sp):
        now = v_recv[it, 1] if it == 0 else prev_v[...]
        new = clipped(now, sp, v_recv[it, 0] - dual_s[it][:scen])
        prev_v[...] = new
        return 2.0 * new - now

    def near_arrived(it):
        @pl.when(has[NEAR])
        def _():
            near_part(it).wait_recv()

    def total_at(it, ch):
        @pl.when(has[FAR])
        def _():
            far_part(it, ch).wait_recv()

        lo = ch * cw
        return own_v[:, lo : lo + cw] + part_recv[it, NEAR, ch] + part_recv[it, FAR, ch]

    per = cw // blk

    def flow_step(it, ch, sp, total):
        lo = ch * cw
        cap = jnp.concatenate(
            [fcap_v[ch * per + i : ch * per + i + 1, :] for i in range(per)], axis=1
        )
        now = flow_s[it, :, lo : lo + cw]
        new = jnp.minimum(jnp.maximum(now + sp * total, -cap), cap)
        fw_own[it, ch] = (2.0 * new - now).astype(bf16)

        @pl.when(has[FAR])
        def _():
            far_flow(it, ch).start()

        flow_s[it + 1, :, lo : lo + cw] = new
        return (new - now) ** 2

    def send_near(it):
        @pl.when(has[NEAR])
        def _():
            near_flow(it).start()

    nt_dims = (((1,), (1,)), ((), ()))

    def joined(get, n):
        return jnp.concatenate([get(ch) for ch in range(n)], axis=1) if n > 1 else get(0)

    def push_own(it):
        mine = jnp.concatenate([fw_own[it, ch] for ch in range(nch)] + [genlow_v[...]], axis=1)
        acc_v[...] = lax.dot_general(a_v[:, at_own:], mine, nt_dims, preferred_element_type=f32)

    def push_near(it):
        @pl.when(has[NEAR])
        def _():
            near_flow(it).wait_recv()

        other = joined(lambda ch: fw_in[it, NEAR, ch], nch)
        acc_v[...] += lax.dot_general(
            a_v[:, at_near:at_own], other, nt_dims, preferred_element_type=f32
        )

    half = nch // 2

    def push_far(it, first, count):
        for ch in range(first, first + count):
            far_flow(it, ch).wait_recv()
        other = joined(lambda ch: fw_in[it, FAR, first + ch], count)
        return lax.dot_general(
            a_v[:, first * cw : (first + count) * cw], other, nt_dims, preferred_element_type=f32
        )

    def push(it, meanwhile, finish):
        push_own(it)
        if half > 0:
            @pl.when(has[FAR])
            def _():
                acc_v[...] += push_far(it, 0, half)

        push_near(it)
        meanwhile()

        @pl.when(has[FAR])
        def _():
            finish(acc_v[...] + push_far(it, half, nch - half))

        @pl.when(jnp.logical_not(has[FAR]))
        def _():
            finish(acc_v[...])

    def ramp_step(it, gbar, prev, sd):
        earlier = prev if cols == scen else jnp.concatenate([prev, gbar[: cols - scen]], axis=0)
        dual = dual_s[it]
        lifted = dual + sd * (gbar - earlier)
        bound = row(caps_v.at[2], n_gens)
        return lifted - sd * jnp.minimum(jnp.maximum(lifted / sd, -bound), bound)

    zero_at = n_tiles + n_gens
    arrived(0, idx_v)
    slot = idx_v[0] * width + (idx_v[1] - (r - 1) * lb)
    down = lax.broadcasted_iota(jnp.int32, (n_tiles, n_tiles), 0)
    across = lax.broadcasted_iota(jnp.int32, (n_tiles, n_tiles), 1)
    upright = jnp.sum(jnp.where(down == across, slot, 0), axis=1, keepdims=True)
    places = lax.broadcasted_iota(jnp.int32, (n_tiles, 128), 1)
    ids = lax.broadcasted_iota(jnp.int32, (n_tiles, 128), 0)
    found = jnp.sum(jnp.where(upright == places, ids - zero_at, 0), axis=0, keepdims=True)
    lane = lax.broadcasted_iota(jnp.int32, (1, 128), 1)
    for g in range(n_gens):
        found = jnp.where(lane == gen_bus[g] * width + 3 * lb + g, n_tiles + g - zero_at, found)
    table_v[...] = jnp.clip(zero_at + found, 0, zero_at)
    to_scalar = pltpu.make_async_copy(table_v, table_s, table_sem.at[0])
    to_scalar.start()

    w1 = jnp.full((1, 1), weight[...], f32)
    arrived(1, price_v)
    set_pt(price_v)
    arrived(2, ramp_v)
    dual_s[0] = ramp_v[...].T
    d_send[0] = dual_s[0][:scen]
    arrived(3, all_tiles)
    to_scalar.wait()
    build(FAR)
    pl.semaphore_wait(barrier, nt - 1 + count[FAR] + count[NEAR])
    if n_stages > 0:
        stage_signal(0)
    dual_copy(0).start()
    for ch in range(0, nch, per_dot):
        far_sums(0, ch)
        send_far(0, ch)
    late_loads()
    build(NEAR)
    pull_near(0)
    build(3)
    pull_gens()
    arrived(4, late_v)
    arrived(5, caps_v)
    gen_s[0] = gen_v[...].T
    gen_pull(0)
    pass_on(0)
    build(2)
    pull_own()
    sd1 = step_scale * w1
    sp1 = step_scale / w1
    for b in range(lb):
        flow_s[0, :, b * blk : (b + 1) * blk] = flow_v[b * blk : (b + 1) * blk, :].T
    arrived(6, fcap_v)
    near_arrived(0)
    primal_acc = jnp.zeros((8, 128), f32)
    for ch in range(nch):
        primal_acc = primal_acc + fold(flow_step(0, ch, sp1, total_at(0, ch)))
        if ch == 0:
            pass_on(1)
    send_near(0)
    for stage in range(2, n_stages - 1):
        pass_on(stage)
    changed, gbar1 = gen_step(0, sp1)
    primal_acc = primal_acc + fold(changed)
    low = lax.broadcasted_iota(jnp.int32, (1, 128), 1) < 64
    primal_row = both_halves(primal_acc)

    def ramp_now():
        prev_copy(0).wait_recv()
        dual_one = ramp_step(0, gbar1, prev_bar(0, sp1), sd1)
        dual_s[1] = dual_one
        change_v[...] = fold((dual_one - dual_s[0]) ** 2)
        dual_copy(0).wait_send()
        d_send[1] = dual_one[:scen]
        dual_copy(1).start()

    def price_now(pushed):
        new = price_v[...] + sd1 * (demand_v[...] - pushed)
        price1_v[...] = new
        dual_row = both_halves(change_v[...] + fold((new - price_v[...]) ** 2))
        ar_s[...] = jnp.where(low, primal_row, dual_row)
        new_low = new.astype(bf16)
        for b in range(bb):
            pt_v[:, b * blk : (b + 1) * blk] = new_low[b * blk : (b + 1) * blk, :].T
        far_sums(1, 0)

    push(0, ramp_now, price_now)

    if n_stages > 0:
        stage_wait(n_stages - 1)
    sent(0)
    others_t = partners(t, nt) + [(0, t)]
    others_r = partners(r, nr) + [(0, r)]
    for k, to_r in others_r:
        for j, to_t in others_t:
            if j or k:
                pltpu.make_async_remote_copy(
                    src_ref=ar_s,
                    dst_ref=ar_r.at[j * nr + k],
                    send_sem=ar_sem.at[0],
                    recv_sem=ar_sem.at[1],
                    device_id={"tm": to_t, "region": to_r},
                    device_id_type=MESH,
                ).start()
    others = ar_r.at[pl.ds(1, nt * nr - 1)]
    send_far(1, 0)
    for ch in range(per_dot, nch, per_dot):
        far_sums(1, ch)
        send_far(1, ch)
    pull_near(1)
    pull_gens()
    prev_copy(0).wait_send()
    gen_pull(1)
    pull_own()
    near_arrived(1)
    pltpu.make_async_copy(others, others, ar_sem.at[1]).wait()
    summed = ar_s[...]
    for at in range(1, nt * nr):
        summed = summed + ar_r[at]
    primal_mean = jnp.sum(jnp.where(low, summed, 0.0), axis=1, keepdims=True) / count_p
    dual_mean = jnp.sum(jnp.where(low, 0.0, summed), axis=1, keepdims=True) / count_d
    w2 = jnp.sqrt(w1 * jnp.sqrt((dual_mean + tiny) / (primal_mean + tiny)))

    sd2 = step_scale * w2
    sp2 = step_scale / w2
    for ch in range(nch):
        flow_step(1, ch, sp2, total_at(1, ch))
    send_near(1)
    _, gbar2 = gen_step(1, sp2)

    def results():
        prev_copy(1).wait_recv()
        o_ramp[...] = ramp_step(1, gbar2, prev_bar(1, sp2), sd2).T
        for b in range(lb):
            o_flow[b * blk : (b + 1) * blk, :] = flow_s[2, :, b * blk : (b + 1) * blk].T
        o_gen[...] = gen_s[2].T

    def price_out(pushed):
        o_price[...] = price1_v[...] + sd2 * (demand_v[...] - pushed)

    push(1, results, price_out)

    dual_copy(1).wait_send()
    prev_copy(1).wait_send()
    sent(1)
    pltpu.make_async_copy(others, others, ar_sem.at[0]).wait()


def shards(
    gen, flow, price, ramp_dual, demand, incid_tiles, tile_bus, tile_line, gen_tiles, gen_bus,
    gen_cost, gen_cap, ramp_cap, flow_cap, weight,
):
    gb, blk, hours, scen = gen.shape
    lb, bb = flow.shape[0], price.shape[0]
    n_tiles = incid_tiles.shape[0]
    cols = hours * scen
    nt, nr = lax.axis_size("tm"), lax.axis_size("region")
    lines, buses, gens = lb * blk, bb * blk, gb * blk
    width = 3 * lb + gb
    nch = lb
    cw = lines // nch
    n_stages, reach = 0, 0
    while reach < nr - 1:
        reach += 2**n_stages
        n_stages += 1

    dims = (
        nt, nr, scen,
        float((gen.size + flow.size) * nt * nr), float((price.size + ramp_dual.size) * nt * nr),
    )
    any_spec = pl.BlockSpec(memory_space=pl.ANY)
    smem_spec = pl.BlockSpec(memory_space=pltpu.SMEM)
    dma = pltpu.SemaphoreType.DMA
    V = pltpu.VMEM
    scratch = [
        V((n_tiles + gb + 1, blk, blk), bf16),
        V((buses, width * blk), bf16),
        V((buses, cols), f32),
        V((gens, cols), f32),
        V((lines + buses + gens, cols), f32),
        V((3, gb, blk), f32),
        V((lb, blk), f32),
        V((cols, buses), bf16),
        V((cols, lines + gens), f32),
        V((buses, cols), f32),
        V((3, cols, lines), f32),
        V((3, cols, gens), f32),
        V((2, cols, gens), f32),
        V((cols, gens), bf16),
        V((2, 2, nch, cols, cw), f32),
        V((2, 2, nch, cols, cw), f32),
        V((2, nch, cols, cw), bf16),
        V((2, 2, nch, cols, cw), bf16),
        V((2, scen, gens), f32),
        V((2, scen, gens), f32),
        V((2, 2, scen, gens), f32),
        V((2, 2, scen, gens), f32),
        V((scen, gens), f32),
        V((1, 128), f32),
        V((nt * nr, 1, 128), f32),
        V((buses, cols), f32),
        V((8, 128), f32),
        V((2, 1, n_tiles), jnp.int32),
        V((1, 128), jnp.int32),
        pltpu.SMEM((1, 128), jnp.int32),
        dma((7,)),
        dma((2,)),
        dma((nch + 1,)),
        dma((2,)),
        dma((nch + 1,)),
        dma((6,)),
        dma((2,)),
        pltpu.SemaphoreType.REGULAR((n_stages,)),
        dma((1,)),
    ]
    vmem_spec = pl.BlockSpec(memory_space=pltpu.VMEM)
    shapes = ((gens, cols), (lines, cols), (buses, cols), (gens, cols))
    outs = pl.pallas_call(
        functools.partial(kernel, dims),
        out_shape=tuple(V(shape, f32) for shape in shapes),
        in_specs=[smem_spec, smem_spec] + [any_spec] * 13,
        out_specs=(vmem_spec,) * 4,
        scratch_shapes=scratch,
        compiler_params=pltpu.CompilerParams(collective_id=0, has_side_effects=True),
    )(
        gen_bus, weight, tile_bus.reshape(1, n_tiles), tile_line.reshape(1, n_tiles), incid_tiles, gen_tiles,
        price.reshape(buses, cols), flow.reshape(lines, cols), gen.reshape(gens, cols),
        ramp_dual.reshape(gens, cols), demand.reshape(buses, cols),
        gen_cost, gen_cap, ramp_cap, flow_cap,
    )
    outs = pl.pallas_call(
        writer,
        out_shape=tuple(jax.ShapeDtypeStruct(shape, f32) for shape in shapes),
        in_specs=[any_spec] * 4,
        out_specs=(any_spec,) * 4,
        scratch_shapes=[dma((4,))],
    )(*(pltpu.with_memory_space_constraint(out, pltpu.VMEM) for out in outs))
    return tuple(
        out.reshape(like.shape) for out, like in zip(outs, (gen, flow, price, ramp_dual))
    )


def solution(mesh):
    field = P("region", None, "tm", None)
    placed = (
        field, field, field, field, field,
        P("region", None, None), P("region"), P("region"), P("region", None, None), P("region"),
        P("region", None), P("region", None), P("region", None), P("region", None), P(),
    )
    return jax.shard_map(
        shards, mesh=mesh, in_specs=placed, out_specs=(field,) * 4, check_vma=False
    )
```

time: 27.8 us -> 25.2 us (0.906)
  the two profiles are of different devices: /device:TPU:0 before, /device:TPU:1 now
where the time goes in v1:
time: 25.2 us; the launch traced here: 25 us
  Pallas kernels  23 us (91%)
  between operations  1.94 us (8%)
    pallas_call x1, Pallas kernels, shards(): pl.pallas_call(functools.partial(kernel, dims), out_shape=tuple((V(shape,...  22.2 us
    pallas_call x1, Pallas kernels, shards(): pl.pallas_call(writer, out_shape=tuple((jax.ShapeDtypeStruct(shape, f32)...  0.86 us

profile of v1, /device:TPU:1, one launch (start us, length us, event | category | flops | bytes accessed | tf_op | source)
XLA Modules:
  0.0 25.0 jit_solution(2135076214922887095)
XLA Ops:
  1.9 22.2 %shard_map.174 = (f32[128,128]{1,0:T(8,128)S(1)}, f32[512,128]{1,0:T(8,128)S(1)}, f32[512,128]{1,0:T(8,128)S(1)}, f32[128,128]{1,0:T(8,128)S(1)}) custom-call(s32[1]{0:T(128)S(6)} %copy.23.gen_bus, f32[]{:T(128)S(6)} %copy.24.weight, s32[1,32]{1,0:T(1,128)} %bitcast.24, s32[1,32]{1,0:T(1,128)} %bitcast.25, bf16[32,128,128]{2,1,0:T(8,128)(2,1)} %tiles.1, ...), custom_call_target="tpu_custom_call" | custom-call | tf_op jit(solution)/shard_map/pallas_call | solution.py:592
  24.1 0.9 %shard_map.175 = (f32[128,128]{1,0:T(8,128)}, f32[512,128]{1,0:T(8,128)}, f32[512,128]{1,0:T(8,128)}, f32[128,128]{1,0:T(8,128)}) custom-call(f32[128,128]{1,0:T(8,128)S(1)} %get-tuple-element.12.refs_0_, f32[512,128]{1,0:T(8,128)S(1)} %get-tuple-element.13.refs_1_, f32[512,128]{1,0:T(8,128)S(1)} %get-tuple-element.14.refs_2_, ...), custom_call_target="tpu_custom_call" | custom-call | tf_op jit(solution)/shard_map/pallas_call | solution.py:605

commit v2 on v1

--- a/solution.py
+++ b/solution.py
@@ -74,8 +74,9 @@
     tiles_v, a_v, price_v, ramp_v, late_v, caps_v, fcap_v,
     pt_v, own_v, price1_v, flow_s, gen_s, dual_s, genlow_v,
     part_send, part_recv, fw_own, fw_in, d_send, d_recv, v_send, v_recv, prev_v,
+    now_send, now_recv, tot_send, tot_recv,
     ar_s, ar_r, acc_v, change_v, idx_v, table_v, table_s,
-    in_sem, ps_sem, pr_sem, fs_sem, fr_sem, tm_sem, ar_sem, ready, table_sem,
+    in_sem, ps_sem, pr_sem, fs_sem, fr_sem, tm_sem, ar_sem, ahead_sem, ready, table_sem,
 ):
     nt, nr, scen, count_p, count_d = dims
     t = lax.axis_index("tm")
@@ -90,6 +91,7 @@
     nch = part_send.shape[2]
     cw = lines // nch
     n_stages = ready.shape[0]
+    early = tot_send.shape[0]
 
     odd = lax.rem(r, 2)
     place = (r - 1 + 2 * odd, r + 1 - 2 * odd)
@@ -196,6 +198,17 @@
             v_send.at[it, parts], v_recv.at[it, parts], tm_sem.at[1], tm_sem.at[4 + it], "tm", t_next
         )
 
+    def now_copy():
+        return remote(
+            now_send, now_recv, ahead_sem.at[0], ahead_sem.at[1], "region", peer[FAR]
+        )
+
+    def total_copy(ch):
+        return remote(
+            tot_send.at[ch], tot_recv.at[ch], ahead_sem.at[2], ahead_sem.at[3 + ch],
+            "region", peer[FAR],
+        )
+
     def sent(it):
         for side in (FAR, NEAR):
             @pl.when(has[side])
@@ -203,6 +216,8 @@
                 ref = part_send.at[it, side]
                 pltpu.make_async_copy(ref, ref, ps_sem.at[side]).wait()
                 ref = fw_own.at[it]
+                if it == 1 and side == FAR:
+                    ref = fw_own.at[it, pl.ds(early, nch - early)]
                 pltpu.make_async_copy(ref, ref, fs_sem.at[side]).wait()
 
     at_near, at_own, at_gens = lines, 2 * lines, 3 * lines
@@ -301,7 +316,7 @@
 
     per = cw // blk
 
-    def flow_step(it, ch, sp, total):
+    def flow_step(it, ch, sp, total, send=True):
         lo = ch * cw
         cap = jnp.concatenate(
             [fcap_v[ch * per + i : ch * per + i + 1, :] for i in range(per)], axis=1
@@ -310,12 +325,26 @@
         new = jnp.minimum(jnp.maximum(now + sp * total, -cap), cap)
         fw_own[it, ch] = (2.0 * new - now).astype(bf16)
 
-        @pl.when(has[FAR])
-        def _():
-            far_flow(it, ch).start()
+        if send:
+            @pl.when(has[FAR])
+            def _():
+                far_flow(it, ch).start()
 
         flow_s[it + 1, :, lo : lo + cw] = new
+        if it == 0 and ch < early:
+            now_send[ch, :cols] = new
+            now_send[ch, cols:] = jnp.broadcast_to(cap, (8, cw))
         return (new - now) ** 2
+
+    def far_flows(sp):
+        now_copy().wait_recv()
+        lows = []
+        for ch in range(early):
+            total_copy(ch).wait_recv()
+            now, cap = now_recv[ch, :cols], now_recv[ch, cols : cols + 1]
+            new = jnp.minimum(jnp.maximum(now + sp * tot_recv[ch], -cap), cap)
+            lows.append((2.0 * new - now).astype(bf16))
+        return jnp.concatenate(lows, axis=1) if early > 1 else lows[0]
 
     def send_near(it):
         @pl.when(has[NEAR])
@@ -341,29 +370,36 @@
             a_v[:, at_near:at_own], other, nt_dims, preferred_element_type=f32
         )
 
-    half = nch // 2
-
-    def push_far(it, first, count):
+    def push_lines(first, low):
+        return lax.dot_general(
+            a_v[:, first * cw : first * cw + low.shape[1]], low, nt_dims, preferred_element_type=f32
+        )
+
+    def far_low(it, first, count):
         for ch in range(first, first + count):
             far_flow(it, ch).wait_recv()
-        other = joined(lambda ch: fw_in[it, FAR, first + ch], count)
-        return lax.dot_general(
-            a_v[:, first * cw : (first + count) * cw], other, nt_dims, preferred_element_type=f32
-        )
-
-    def push(it, meanwhile, finish):
+        return joined(lambda ch: fw_in[it, FAR, first + ch], count)
+
+    def push(it, ahead, meanwhile, early_low, finish):
+        def far_first():
+            if ahead > 0:
+                @pl.when(has[FAR])
+                def _():
+                    acc_v[...] += push_lines(0, early_low())
+
         push_own(it)
-        if half > 0:
-            @pl.when(has[FAR])
-            def _():
-                acc_v[...] += push_far(it, 0, half)
-
-        push_near(it)
-        meanwhile()
+        if it == 0:
+            far_first()
+            push_near(it)
+            meanwhile()
+        else:
+            far_first()
+            meanwhile()
+            push_near(it)
 
         @pl.when(has[FAR])
         def _():
-            finish(acc_v[...] + push_far(it, half, nch - half))
+            finish(acc_v[...] + push_lines(ahead, far_low(it, ahead, nch - ahead)))
 
         @pl.when(jnp.logical_not(has[FAR]))
         def _():
@@ -431,6 +467,11 @@
         primal_acc = primal_acc + fold(flow_step(0, ch, sp1, total_at(0, ch)))
         if ch == 0:
             pass_on(1)
+    if early > 0:
+        @pl.when(has[FAR])
+        def _():
+            now_copy().start()
+
     send_near(0)
     for stage in range(2, n_stages - 1):
         pass_on(stage)
@@ -458,7 +499,7 @@
             pt_v[:, b * blk : (b + 1) * blk] = new_low[b * blk : (b + 1) * blk, :].T
         far_sums(1, 0)
 
-    push(0, ramp_now, price_now)
+    push(0, nch // 2, ramp_now, lambda: far_low(0, 0, nch // 2), price_now)
 
     if n_stages > 0:
         stage_wait(n_stages - 1)
@@ -487,6 +528,13 @@
     gen_pull(1)
     pull_own()
     near_arrived(1)
+    for ch in range(early):
+        tot_send[ch] = total_at(1, ch)
+
+        @pl.when(has[FAR])
+        def _():
+            total_copy(ch).start()
+
     pltpu.make_async_copy(others, others, ar_sem.at[1]).wait()
     summed = ar_s[...]
     for at in range(1, nt * nr):
@@ -497,8 +545,10 @@
 
     sd2 = step_scale * w2
     sp2 = step_scale / w2
-    for ch in range(nch):
+    for ch in range(early, nch):
         flow_step(1, ch, sp2, total_at(1, ch))
+    for ch in range(early):
+        flow_step(1, ch, sp2, tot_send[ch], send=False)
     send_near(1)
     _, gbar2 = gen_step(1, sp2)
 
@@ -512,11 +562,17 @@
     def price_out(pushed):
         o_price[...] = price1_v[...] + sd2 * (demand_v[...] - pushed)
 
-    push(1, results, price_out)
+    push(1, early, results, lambda: far_flows(sp2), price_out)
 
     dual_copy(1).wait_send()
     prev_copy(1).wait_send()
     sent(1)
+    if early > 0:
+        @pl.when(has[FAR])
+        def _():
+            now_copy().wait_send()
+            pltpu.make_async_copy(tot_send, tot_send, ahead_sem.at[2]).wait()
+
     pltpu.make_async_copy(others, others, ar_sem.at[0]).wait()
 
 
@@ -532,6 +588,7 @@
     lines, buses, gens = lb * blk, bb * blk, gb * blk
     width = 3 * lb + gb
     nch = lb
+    early = nch - 1
     cw = lines // nch
     n_stages, reach = 0, 0
     while reach < nr - 1:
@@ -570,6 +627,10 @@
         V((2, 2, scen, gens), f32),
         V((2, 2, scen, gens), f32),
         V((scen, gens), f32),
+        V((early, cols + 8, cw), f32),
+        V((early, cols + 8, cw), f32),
+        V((early, cols, cw), f32),
+        V((early, cols, cw), f32),
         V((1, 128), f32),
         V((nt * nr, 1, 128), f32),
         V((buses, cols), f32),
@@ -584,6 +645,7 @@
         dma((nch + 1,)),
         dma((6,)),
         dma((2,)),
+        dma((3 + early,)),
         pltpu.SemaphoreType.REGULAR((n_stages,)),
         dma((1,)),
     ]

time: 25.2 us -> 24.4 us (0.968)
  Pallas kernels: 23 us -> 22.3 us
    pallas_call x1, Pallas kernels: 22.2 us -> 21.4 us  [shards(): pl.pallas_call(functools.partial(kernel, dims), out_shape=tuple((V(shape,...]
where the time goes in v2:
time: 24.4 us; the launch traced here: 24.2 us
  Pallas kernels  22.3 us (91%)
  between operations  1.94 us (8%)
    pallas_call x1, Pallas kernels, shards(): pl.pallas_call(functools.partial(kernel, dims), out_shape=tuple((V(shape,...  21.4 us
    pallas_call x1, Pallas kernels, shards(): pl.pallas_call(writer, out_shape=tuple((jax.ShapeDtypeStruct(shape, f32)...  0.86 us

profile of v2, /device:TPU:1, one launch (start us, length us, event | category | flops | bytes accessed | tf_op | source)
XLA Modules:
  0.0 24.2 jit_solution(13658685041789460694)
XLA Ops:
  1.9 21.4 %shard_map.174 = (f32[128,128]{1,0:T(8,128)S(1)}, f32[512,128]{1,0:T(8,128)S(1)}, f32[512,128]{1,0:T(8,128)S(1)}, f32[128,128]{1,0:T(8,128)S(1)}) custom-call(s32[1]{0:T(128)S(6)} %copy.23.gen_bus, f32[]{:T(128)S(6)} %copy.24.weight, s32[1,32]{1,0:T(1,128)} %bitcast.24, s32[1,32]{1,0:T(1,128)} %bitcast.25, bf16[32,128,128]{2,1,0:T(8,128)(2,1)} %tiles.1, ...), custom_call_target="tpu_custom_call" | custom-call | tf_op jit(solution)/shard_map/pallas_call | solution.py:654
  23.3 0.9 %shard_map.175 = (f32[128,128]{1,0:T(8,128)}, f32[512,128]{1,0:T(8,128)}, f32[512,128]{1,0:T(8,128)}, f32[128,128]{1,0:T(8,128)}) custom-call(f32[128,128]{1,0:T(8,128)S(1)} %get-tuple-element.12.refs_0_, f32[512,128]{1,0:T(8,128)S(1)} %get-tuple-element.13.refs_1_, f32[512,128]{1,0:T(8,128)S(1)} %get-tuple-element.14.refs_2_, ...), custom_call_target="tpu_custom_call" | custom-call | tf_op jit(solution)/shard_map/pallas_call | solution.py:667

commit v3 on v2

--- a/solution.py
+++ b/solution.py
@@ -60,7 +60,7 @@
 
 def partners(x, n):
     if n & (n - 1) == 0:
-        return [(m, flip(x, m)) for m in range(n - 1, 0, -1)]
+        return [(m, flip(x, m)) for m in [*range(n // 2, n), *range(n // 2 - 1, 0, -1)]]
     return [(m, lax.rem(x + m, n)) for m in range(1, n)]
 
 
@@ -71,12 +71,12 @@
     dims,
     gen_bus, weight, tile_bus, tile_line, tiles, gtiles, price, flow, gen, ramp, demand, cost, gcap, rcap, fcap,
     o_gen, o_flow, o_price, o_ramp,
-    tiles_v, a_v, price_v, ramp_v, late_v, caps_v, fcap_v,
+    tiles_v, a_v, first_v, late_v, caps_v, fcap_v,
     pt_v, own_v, price1_v, flow_s, gen_s, dual_s, genlow_v,
     part_send, part_recv, fw_own, fw_in, d_send, d_recv, v_send, v_recv, prev_v,
     now_send, now_recv, tot_send, tot_recv,
     ar_s, ar_r, acc_v, change_v, idx_v, table_v, table_s,
-    in_sem, ps_sem, pr_sem, fs_sem, fr_sem, tm_sem, ar_sem, ahead_sem, ready, table_sem,
+    in_sem, ps_sem, pr_sem, fs_sem, fr_sem, tm_sem, ar_sem, ahead_sem, ready,
 ):
     nt, nr, scen, count_p, count_d = dims
     t = lax.axis_index("tm")
@@ -87,7 +87,6 @@
     buses = price.shape[0]
     lb, bb = lines // blk, buses // blk
     width = 3 * lb + n_gens
-    gens = gen.shape[0]
     nch = part_send.shape[2]
     cw = lines // nch
     n_stages = ready.shape[0]
@@ -143,17 +142,18 @@
 
     load(0, (tile_bus, idx_v.at[0]), (tile_line, idx_v.at[1]))
     all_tiles = tiles_v.at[pl.ds(0, n_tiles + n_gens)]
-    load(1, (price, price_v))
-    load(2, (ramp, ramp_v))
-    load(3, (tiles, tiles_v.at[pl.ds(0, n_tiles)]), (gtiles, tiles_v.at[pl.ds(n_tiles, n_gens)]))
+    gens = gen.shape[0]
+    price_v, ramp_v = first_v.at[pl.ds(0, buses)], first_v.at[pl.ds(buses, gens)]
+    load(1, (price, price_v), (ramp, ramp_v))
+    load(2, (tiles, tiles_v.at[pl.ds(0, n_tiles)]), (gtiles, tiles_v.at[pl.ds(n_tiles, n_gens)]))
     flow_v = late_v.at[pl.ds(0, lines)]
     demand_v = late_v.at[pl.ds(lines, buses)]
     gen_v = late_v.at[pl.ds(lines + buses, gens)]
 
     def late_loads():
-        load(4, (flow, flow_v), (demand, demand_v), (gen, gen_v))
-        load(5, (cost, caps_v.at[0]), (gcap, caps_v.at[1]), (rcap, caps_v.at[2]))
-        load(6, (fcap, fcap_v))
+        load(0, (flow, flow_v), (demand, demand_v), (gen, gen_v))
+        load(1, (cost, caps_v.at[0]), (gcap, caps_v.at[1]), (rcap, caps_v.at[2]))
+        load(2, (fcap, fcap_v))
 
     tiles_v[n_tiles + n_gens] = jnp.zeros((blk, blk), bf16)
 
@@ -205,7 +205,7 @@
 
     def total_copy(ch):
         return remote(
-            tot_send.at[ch], tot_recv.at[ch], ahead_sem.at[2], ahead_sem.at[3 + ch],
+            tot_send.at[ch], tot_recv.at[ch], ahead_sem.at[0], fr_sem.at[ch],
             "region", peer[FAR],
         )
 
@@ -336,15 +336,11 @@
             now_send[ch, cols:] = jnp.broadcast_to(cap, (8, cw))
         return (new - now) ** 2
 
-    def far_flows(sp):
-        now_copy().wait_recv()
-        lows = []
-        for ch in range(early):
-            total_copy(ch).wait_recv()
-            now, cap = now_recv[ch, :cols], now_recv[ch, cols : cols + 1]
-            new = jnp.minimum(jnp.maximum(now + sp * tot_recv[ch], -cap), cap)
-            lows.append((2.0 * new - now).astype(bf16))
-        return jnp.concatenate(lows, axis=1) if early > 1 else lows[0]
+    def ahead_low(sp, ch):
+        total_copy(ch).wait_recv()
+        now, cap = now_recv[ch, :cols], now_recv[ch, cols : cols + 1]
+        new = jnp.minimum(jnp.maximum(now + sp * tot_recv[ch], -cap), cap)
+        return (2.0 * new - now).astype(bf16)
 
     def send_near(it):
         @pl.when(has[NEAR])
@@ -375,31 +371,36 @@
             a_v[:, first * cw : first * cw + low.shape[1]], low, nt_dims, preferred_element_type=f32
         )
 
-    def far_low(it, first, count):
+    half = nch // 2
+
+    def far_low(it, sp, first, count):
+        lows = []
         for ch in range(first, first + count):
-            far_flow(it, ch).wait_recv()
-        return joined(lambda ch: fw_in[it, FAR, first + ch], count)
-
-    def push(it, ahead, meanwhile, early_low, finish):
-        def far_first():
-            if ahead > 0:
-                @pl.when(has[FAR])
-                def _():
-                    acc_v[...] += push_lines(0, early_low())
-
+            if it == 1 and ch < early:
+                lows.append(ahead_low(sp, ch))
+            else:
+                far_flow(it, ch).wait_recv()
+                lows.append(fw_in[it, FAR, ch])
+        return jnp.concatenate(lows, axis=1) if count > 1 else lows[0]
+
+    def push(it, sp, meanwhile, finish):
         push_own(it)
+        if it == 1:
+            meanwhile()
+        if half > 0:
+            @pl.when(has[FAR])
+            def _():
+                if it == 1:
+                    now_copy().wait_recv()
+                acc_v[...] += push_lines(0, far_low(it, sp, 0, half))
+
+        push_near(it)
         if it == 0:
-            far_first()
-            push_near(it)
             meanwhile()
-        else:
-            far_first()
-            meanwhile()
-            push_near(it)
 
         @pl.when(has[FAR])
         def _():
-            finish(acc_v[...] + push_lines(ahead, far_low(it, ahead, nch - ahead)))
+            finish(acc_v[...] + push_lines(half, far_low(it, sp, half, nch - half)))
 
         @pl.when(jnp.logical_not(has[FAR]))
         def _():
@@ -425,16 +426,15 @@
     for g in range(n_gens):
         found = jnp.where(lane == gen_bus[g] * width + 3 * lb + g, n_tiles + g - zero_at, found)
     table_v[...] = jnp.clip(zero_at + found, 0, zero_at)
-    to_scalar = pltpu.make_async_copy(table_v, table_s, table_sem.at[0])
+    to_scalar = pltpu.make_async_copy(table_v, table_s, in_sem.at[0])
     to_scalar.start()
 
     w1 = jnp.full((1, 1), weight[...], f32)
-    arrived(1, price_v)
+    arrived(1, first_v)
     set_pt(price_v)
-    arrived(2, ramp_v)
     dual_s[0] = ramp_v[...].T
     d_send[0] = dual_s[0][:scen]
-    arrived(3, all_tiles)
+    arrived(2, all_tiles)
     to_scalar.wait()
     build(FAR)
     pl.semaphore_wait(barrier, nt - 1 + count[FAR] + count[NEAR])
@@ -449,8 +449,8 @@
     pull_near(0)
     build(3)
     pull_gens()
-    arrived(4, late_v)
-    arrived(5, caps_v)
+    arrived(0, late_v)
+    arrived(1, caps_v)
     gen_s[0] = gen_v[...].T
     gen_pull(0)
     pass_on(0)
@@ -460,7 +460,7 @@
     sp1 = step_scale / w1
     for b in range(lb):
         flow_s[0, :, b * blk : (b + 1) * blk] = flow_v[b * blk : (b + 1) * blk, :].T
-    arrived(6, fcap_v)
+    arrived(2, fcap_v)
     near_arrived(0)
     primal_acc = jnp.zeros((8, 128), f32)
     for ch in range(nch):
@@ -494,12 +494,8 @@
         price1_v[...] = new
         dual_row = both_halves(change_v[...] + fold((new - price_v[...]) ** 2))
         ar_s[...] = jnp.where(low, primal_row, dual_row)
-        new_low = new.astype(bf16)
-        for b in range(bb):
-            pt_v[:, b * blk : (b + 1) * blk] = new_low[b * blk : (b + 1) * blk, :].T
-        far_sums(1, 0)
-
-    push(0, nch // 2, ramp_now, lambda: far_low(0, 0, nch // 2), price_now)
+
+    push(0, sp1, ramp_now, price_now)
 
     if n_stages > 0:
         stage_wait(n_stages - 1)
@@ -518,8 +514,8 @@
                     device_id_type=MESH,
                 ).start()
     others = ar_r.at[pl.ds(1, nt * nr - 1)]
-    send_far(1, 0)
-    for ch in range(per_dot, nch, per_dot):
+    set_pt(price1_v)
+    for ch in range(0, nch, per_dot):
         far_sums(1, ch)
         send_far(1, ch)
     pull_near(1)
@@ -533,6 +529,8 @@
 
         @pl.when(has[FAR])
         def _():
+            if ch == 0:
+                now_copy().wait_send()
             total_copy(ch).start()
 
     pltpu.make_async_copy(others, others, ar_sem.at[1]).wait()
@@ -562,7 +560,7 @@
     def price_out(pushed):
         o_price[...] = price1_v[...] + sd2 * (demand_v[...] - pushed)
 
-    push(1, early, results, lambda: far_flows(sp2), price_out)
+    push(1, sp2, results, price_out)
 
     dual_copy(1).wait_send()
     prev_copy(1).wait_send()
@@ -570,8 +568,7 @@
     if early > 0:
         @pl.when(has[FAR])
         def _():
-            now_copy().wait_send()
-            pltpu.make_async_copy(tot_send, tot_send, ahead_sem.at[2]).wait()
+            pltpu.make_async_copy(tot_send, tot_send, ahead_sem.at[0]).wait()
 
     pltpu.make_async_copy(others, others, ar_sem.at[0]).wait()
 
@@ -588,7 +585,7 @@
     lines, buses, gens = lb * blk, bb * blk, gb * blk
     width = 3 * lb + gb
     nch = lb
-    early = nch - 1
+    early = nch // 2
     cw = lines // nch
     n_stages, reach = 0, 0
     while reach < nr - 1:
@@ -606,8 +603,7 @@
     scratch = [
         V((n_tiles + gb + 1, blk, blk), bf16),
         V((buses, width * blk), bf16),
-        V((buses, cols), f32),
-        V((gens, cols), f32),
+        V((buses + gens, cols), f32),
         V((lines + buses + gens, cols), f32),
         V((3, gb, blk), f32),
         V((lb, blk), f32),
@@ -638,16 +634,15 @@
         V((2, 1, n_tiles), jnp.int32),
         V((1, 128), jnp.int32),
         pltpu.SMEM((1, 128), jnp.int32),
-        dma((7,)),
+        dma((3,)),
         dma((2,)),
         dma((nch + 1,)),
         dma((2,)),
         dma((nch + 1,)),
         dma((6,)),
         dma((2,)),
-        dma((3 + early,)),
+        dma((2,)),
         pltpu.SemaphoreType.REGULAR((n_stages,)),
-        dma((1,)),
     ]
     vmem_spec = pl.BlockSpec(memory_space=pltpu.VMEM)
     shapes = ((gens, cols), (lines, cols), (buses, cols), (gens, cols))

time: 24.4 us -> 24.1 us (0.988)
  Pallas kernels: 22.3 us -> 22 us
    pallas_call x1, Pallas kernels: 21.4 us -> 21.1 us  [shards(): pl.pallas_call(functools.partial(kernel, dims), out_shape=tuple((V(shape,...]
where the time goes in v3:
time: 24.1 us; the launch traced here: 23.9 us
  Pallas kernels  22 us (91%)
  between operations  1.94 us (8%)
    pallas_call x1, Pallas kernels, shards(): pl.pallas_call(functools.partial(kernel, dims), out_shape=tuple((V(shape,...  21.1 us
    pallas_call x1, Pallas kernels, shards(): pl.pallas_call(writer, out_shape=tuple((jax.ShapeDtypeStruct(shape, f32)...  0.86 us

profile of v3, /device:TPU:1, one launch (start us, length us, event | category | flops | bytes accessed | tf_op | source)
XLA Modules:
  0.0 23.9 jit_solution(10172639568813202007)
XLA Ops:
  1.9 21.1 %shard_map.174 = (f32[128,128]{1,0:T(8,128)S(1)}, f32[512,128]{1,0:T(8,128)S(1)}, f32[512,128]{1,0:T(8,128)S(1)}, f32[128,128]{1,0:T(8,128)S(1)}) custom-call(s32[1]{0:T(128)S(6)} %copy.23.gen_bus, f32[]{:T(128)S(6)} %copy.24.weight, s32[1,32]{1,0:T(1,128)} %bitcast.24, s32[1,32]{1,0:T(1,128)} %bitcast.25, bf16[32,128,128]{2,1,0:T(8,128)(2,1)} %tiles.1, ...), custom_call_target="tpu_custom_call" | custom-call | tf_op jit(solution)/shard_map/pallas_call | solution.py:649
  23.1 0.9 %shard_map.175 = (f32[128,128]{1,0:T(8,128)}, f32[512,128]{1,0:T(8,128)}, f32[512,128]{1,0:T(8,128)}, f32[128,128]{1,0:T(8,128)}) custom-call(f32[128,128]{1,0:T(8,128)S(1)} %get-tuple-element.12.refs_0_, f32[512,128]{1,0:T(8,128)S(1)} %get-tuple-element.13.refs_1_, f32[512,128]{1,0:T(8,128)S(1)} %get-tuple-element.14.refs_2_, ...), custom_call_target="tpu_custom_call" | custom-call | tf_op jit(solution)/shard_map/pallas_call | solution.py:662

commit v4 on v3

--- a/solution.py
+++ b/solution.py
@@ -74,11 +74,11 @@
     tiles_v, a_v, first_v, late_v, caps_v, fcap_v,
     pt_v, own_v, price1_v, flow_s, gen_s, dual_s, genlow_v,
     part_send, part_recv, fw_own, fw_in, d_send, d_recv, v_send, v_recv, prev_v,
-    now_send, now_recv, tot_send, tot_recv,
+    ahead_send, ahead_recv, state_send, state_recv, far_new,
     ar_s, ar_r, acc_v, change_v, idx_v, table_v, table_s,
     in_sem, ps_sem, pr_sem, fs_sem, fr_sem, tm_sem, ar_sem, ahead_sem, ready,
 ):
-    nt, nr, scen, count_p, count_d = dims
+    nt, nr, scen, count_p, count_d, early = dims
     t = lax.axis_index("tm")
     r = lax.axis_index("region")
     n_tiles, blk, _ = tiles.shape
@@ -90,7 +90,8 @@
     nch = part_send.shape[2]
     cw = lines // nch
     n_stages = ready.shape[0]
-    early = tot_send.shape[0]
+    known = min(early, 1)
+    ahead_rows = (2 * cols + 8, early * cols)
 
     odd = lax.rem(r, 2)
     place = (r - 1 + 2 * odd, r + 1 - 2 * odd)
@@ -168,7 +169,8 @@
     def far_part(it, ch):
         return remote(
             part_send.at[it, FAR, ch], part_recv.at[it, FAR, ch],
-            ps_sem.at[FAR], pr_sem.at[ch], "region", peer[FAR],
+            ps_sem.at[FAR], pr_sem.at[nch + 1 if it == 1 and ch >= nch - known else ch],
+            "region", peer[FAR],
         )
 
     def near_part(it):
@@ -198,15 +200,16 @@
             v_send.at[it, parts], v_recv.at[it, parts], tm_sem.at[1], tm_sem.at[4 + it], "tm", t_next
         )
 
-    def now_copy():
+    def ahead_copy(it):
+        rows = pl.ds(0, ahead_rows[it])
         return remote(
-            now_send, now_recv, ahead_sem.at[0], ahead_sem.at[1], "region", peer[FAR]
-        )
-
-    def total_copy(ch):
+            ahead_send.at[it, rows], ahead_recv.at[it, rows],
+            ahead_sem.at[0], ahead_sem.at[1 + it], "region", peer[FAR],
+        )
+
+    def state_copy():
         return remote(
-            tot_send.at[ch], tot_recv.at[ch], ahead_sem.at[0], fr_sem.at[ch],
-            "region", peer[FAR],
+            state_send, state_recv, ahead_sem.at[0], ahead_sem.at[3], "region", peer[FAR]
         )
 
     def sent(it):
@@ -216,8 +219,8 @@
                 ref = part_send.at[it, side]
                 pltpu.make_async_copy(ref, ref, ps_sem.at[side]).wait()
                 ref = fw_own.at[it]
-                if it == 1 and side == FAR:
-                    ref = fw_own.at[it, pl.ds(early, nch - early)]
+                if side == FAR:
+                    ref = fw_own.at[it, pl.ds(0, nch - (known, early)[it])]
                 pltpu.make_async_copy(ref, ref, fs_sem.at[side]).wait()
 
     at_near, at_own, at_gens = lines, 2 * lines, 3 * lines
@@ -316,30 +319,69 @@
 
     per = cw // blk
 
-    def flow_step(it, ch, sp, total, send=True):
+    def caps_of(ch):
+        return jnp.concatenate(
+            [fcap_v[ch * per + i : ch * per + i + 1, :] for i in range(per)], axis=1
+        )
+
+    def stepped(now, sp, total, cap):
+        return jnp.minimum(jnp.maximum(now + sp * total, -cap), cap)
+
+    def flow_step(it, ch, sp, total):
         lo = ch * cw
-        cap = jnp.concatenate(
-            [fcap_v[ch * per + i : ch * per + i + 1, :] for i in range(per)], axis=1
-        )
         now = flow_s[it, :, lo : lo + cw]
-        new = jnp.minimum(jnp.maximum(now + sp * total, -cap), cap)
+        new = stepped(now, sp, total, caps_of(ch))
         fw_own[it, ch] = (2.0 * new - now).astype(bf16)
 
-        if send:
+        if ch < nch - (known, early)[it]:
             @pl.when(has[FAR])
             def _():
                 far_flow(it, ch).start()
 
         flow_s[it + 1, :, lo : lo + cw] = new
-        if it == 0 and ch < early:
-            now_send[ch, :cols] = new
-            now_send[ch, cols:] = jnp.broadcast_to(cap, (8, cw))
         return (new - now) ** 2
 
-    def ahead_low(sp, ch):
-        total_copy(ch).wait_recv()
-        now, cap = now_recv[ch, :cols], now_recv[ch, cols : cols + 1]
-        new = jnp.minimum(jnp.maximum(now + sp * tot_recv[ch], -cap), cap)
+    def put_state(ref, it, ch):
+        ref[:cols] = flow_s[it, :, ch * cw : (ch + 1) * cw]
+        ref[cols:] = jnp.broadcast_to(caps_of(ch), (8, cw))
+
+    def ahead_start(it):
+        count = (known, early)[it]
+        for s in range(count):
+            lo = (nch - count + s) * cw
+            ahead_send[it, s * cols : (s + 1) * cols] = (
+                own_v[:, lo : lo + cw] + part_recv[it, NEAR, nch - count + s]
+            )
+        if it == 0:
+            put_state(ahead_send.at[0, pl.ds(cols, cols + 8)], 0, nch - 1)
+
+        @pl.when(has[FAR])
+        def _():
+            if it == 1:
+                (state_copy() if early > known else ahead_copy(0)).wait_send()
+            ahead_copy(it).start()
+
+    def state_start():
+        for s in range(early - known):
+            put_state(state_send.at[s], 1, nch - early + s)
+
+        @pl.when(has[FAR])
+        def _():
+            ahead_copy(0).wait_send()
+            state_copy().start()
+
+    def ahead_low(it, sp, ch):
+        count = (known, early)[it]
+        s = ch - (nch - count)
+        total = ahead_recv[it, s * cols : (s + 1) * cols] + part_send[it, FAR, ch]
+        if it == 0 or ch >= nch - known:
+            now = far_new[...] if it == 1 else ahead_recv[0, cols : 2 * cols]
+            cap = ahead_recv[0, 2 * cols : 2 * cols + 1]
+        else:
+            now, cap = state_recv[s, :cols], state_recv[s, cols : cols + 1]
+        new = stepped(now, sp, total, cap)
+        if it == 0:
+            far_new[...] = new
         return (2.0 * new - now).astype(bf16)
 
     def send_near(it):
@@ -366,33 +408,39 @@
             a_v[:, at_near:at_own], other, nt_dims, preferred_element_type=f32
         )
 
-    def push_lines(first, low):
-        return lax.dot_general(
-            a_v[:, first * cw : first * cw + low.shape[1]], low, nt_dims, preferred_element_type=f32
-        )
-
-    half = nch // 2
-
-    def far_low(it, sp, first, count):
+    def push_far(it, sp, chunks):
         lows = []
-        for ch in range(first, first + count):
-            if it == 1 and ch < early:
-                lows.append(ahead_low(sp, ch))
+        for ch in chunks:
+            if ch >= nch - (known, early)[it]:
+                lows.append(ahead_low(it, sp, ch))
             else:
                 far_flow(it, ch).wait_recv()
                 lows.append(fw_in[it, FAR, ch])
-        return jnp.concatenate(lows, axis=1) if count > 1 else lows[0]
+        wide = [a_v[:, ch * cw : (ch + 1) * cw] for ch in chunks]
+        many = len(chunks) > 1
+        return lax.dot_general(
+            jnp.concatenate(wide, axis=1) if many else wide[0],
+            jnp.concatenate(lows, axis=1) if many else lows[0],
+            nt_dims, preferred_element_type=f32,
+        )
 
     def push(it, sp, meanwhile, finish):
+        count = (known, early)[it]
+        more = max(nch // 2 - count, 0)
+        first = [*range(nch - count, nch), *range(more)]
+        last = [*range(more, nch - count)]
+        if it == 0 and early > known:
+            state_start()
         push_own(it)
         if it == 1:
             meanwhile()
-        if half > 0:
+        if count > 0:
             @pl.when(has[FAR])
             def _():
-                if it == 1:
-                    now_copy().wait_recv()
-                acc_v[...] += push_lines(0, far_low(it, sp, 0, half))
+                ahead_copy(it).wait_recv()
+                if it == 1 and early > known:
+                    state_copy().wait_recv()
+                acc_v[...] += push_far(it, sp, first)
 
         push_near(it)
         if it == 0:
@@ -400,7 +448,7 @@
 
         @pl.when(has[FAR])
         def _():
-            finish(acc_v[...] + push_lines(half, far_low(it, sp, half, nch - half)))
+            finish(acc_v[...] + push_far(it, sp, last))
 
         @pl.when(jnp.logical_not(has[FAR]))
         def _():
@@ -462,16 +510,13 @@
         flow_s[0, :, b * blk : (b + 1) * blk] = flow_v[b * blk : (b + 1) * blk, :].T
     arrived(2, fcap_v)
     near_arrived(0)
+    if early > 0:
+        ahead_start(0)
     primal_acc = jnp.zeros((8, 128), f32)
     for ch in range(nch):
         primal_acc = primal_acc + fold(flow_step(0, ch, sp1, total_at(0, ch)))
         if ch == 0:
             pass_on(1)
-    if early > 0:
-        @pl.when(has[FAR])
-        def _():
-            now_copy().start()
-
     send_near(0)
     for stage in range(2, n_stages - 1):
         pass_on(stage)
@@ -524,15 +569,8 @@
     gen_pull(1)
     pull_own()
     near_arrived(1)
-    for ch in range(early):
-        tot_send[ch] = total_at(1, ch)
-
-        @pl.when(has[FAR])
-        def _():
-            if ch == 0:
-                now_copy().wait_send()
-            total_copy(ch).start()
-
+    if early > 0:
+        ahead_start(1)
     pltpu.make_async_copy(others, others, ar_sem.at[1]).wait()
     summed = ar_s[...]
     for at in range(1, nt * nr):
@@ -543,10 +581,8 @@
 
     sd2 = step_scale * w2
     sp2 = step_scale / w2
-    for ch in range(early, nch):
+    for ch in range(nch):
         flow_step(1, ch, sp2, total_at(1, ch))
-    for ch in range(early):
-        flow_step(1, ch, sp2, tot_send[ch], send=False)
     send_near(1)
     _, gbar2 = gen_step(1, sp2)
 
@@ -568,7 +604,7 @@
     if early > 0:
         @pl.when(has[FAR])
         def _():
-            pltpu.make_async_copy(tot_send, tot_send, ahead_sem.at[0]).wait()
+            ahead_copy(1).wait_send()
 
     pltpu.make_async_copy(others, others, ar_sem.at[0]).wait()
 
@@ -586,6 +622,7 @@
     width = 3 * lb + gb
     nch = lb
     early = nch // 2
+    ahead_rows = max(2 * cols + 8, early * cols)
     cw = lines // nch
     n_stages, reach = 0, 0
     while reach < nr - 1:
@@ -594,7 +631,7 @@
 
     dims = (
         nt, nr, scen,
-        float((gen.size + flow.size) * nt * nr), float((price.size + ramp_dual.size) * nt * nr),
+        float((gen.size + flow.size) * nt * nr), float((price.size + ramp_dual.size) * nt * nr), early,
     )
     any_spec = pl.BlockSpec(memory_space=pl.ANY)
     smem_spec = pl.BlockSpec(memory_space=pltpu.SMEM)
@@ -623,10 +660,11 @@
         V((2, 2, scen, gens), f32),
         V((2, 2, scen, gens), f32),
         V((scen, gens), f32),
-        V((early, cols + 8, cw), f32),
-        V((early, cols + 8, cw), f32),
-        V((early, cols, cw), f32),
-        V((early, cols, cw), f32),
+        V((2, ahead_rows, cw), f32),
+        V((2, ahead_rows, cw), f32),
+        V((max(early - 1, 1), cols + 8, cw), f32),
+        V((max(early - 1, 1), cols + 8, cw), f32),
+        V((cols, cw), f32),
         V((1, 128), f32),
         V((nt * nr, 1, 128), f32),
         V((buses, cols), f32),
@@ -636,12 +674,12 @@
         pltpu.SMEM((1, 128), jnp.int32),
         dma((3,)),
         dma((2,)),
-        dma((nch + 1,)),
+        dma((nch + 2,)),
         dma((2,)),
         dma((nch + 1,)),
         dma((6,)),
         dma((2,)),
-        dma((2,)),
+        dma((4,)),
         pltpu.SemaphoreType.REGULAR((n_stages,)),
     ]
     vmem_spec = pl.BlockSpec(memory_space=pltpu.VMEM)

time: 24.1 us -> 23.5 us (0.975)
  Pallas kernels: 22 us -> 21.4 us
    pallas_call x1, Pallas kernels: 21.1 us -> 20.5 us  [shards(): pl.pallas_call(functools.partial(kernel, dims), out_shape=tuple((V(shape,...]
where the time goes in v4:
time: 23.5 us; the launch traced here: 23.3 us
  Pallas kernels  21.4 us (91%)
  between operations  1.94 us (8%)
    pallas_call x1, Pallas kernels, shards(): pl.pallas_call(functools.partial(kernel, dims), out_shape=tuple((V(shape,...  20.5 us
    pallas_call x1, Pallas kernels, shards(): pl.pallas_call(writer, out_shape=tuple((jax.ShapeDtypeStruct(shape, f32)...  0.86 us

profile of v4, /device:TPU:1, one launch (start us, length us, event | category | flops | bytes accessed | tf_op | source)
XLA Modules:
  0.0 23.3 jit_solution(1083889061310722583)
XLA Ops:
  1.9 20.5 %shard_map.174 = (f32[128,128]{1,0:T(8,128)S(1)}, f32[512,128]{1,0:T(8,128)S(1)}, f32[512,128]{1,0:T(8,128)S(1)}, f32[128,128]{1,0:T(8,128)S(1)}) custom-call(s32[1]{0:T(128)S(6)} %copy.23.gen_bus, f32[]{:T(128)S(6)} %copy.24.weight, s32[1,32]{1,0:T(1,128)} %bitcast.24, s32[1,32]{1,0:T(1,128)} %bitcast.25, bf16[32,128,128]{2,1,0:T(8,128)(2,1)} %tiles.1, ...), custom_call_target="tpu_custom_call" | custom-call | tf_op jit(solution)/shard_map/pallas_call | solution.py:687
  22.5 0.9 %shard_map.175 = (f32[128,128]{1,0:T(8,128)}, f32[512,128]{1,0:T(8,128)}, f32[512,128]{1,0:T(8,128)}, f32[128,128]{1,0:T(8,128)}) custom-call(f32[128,128]{1,0:T(8,128)S(1)} %get-tuple-element.12.refs_0_, f32[512,128]{1,0:T(8,128)S(1)} %get-tuple-element.13.refs_1_, f32[512,128]{1,0:T(8,128)S(1)} %get-tuple-element.14.refs_2_, ...), custom_call_target="tpu_custom_call" | custom-call | tf_op jit(solution)/shard_map/pallas_call | solution.py:700

commit v5 on v4

--- a/solution.py
+++ b/solution.py
@@ -74,7 +74,7 @@
     tiles_v, a_v, first_v, late_v, caps_v, fcap_v,
     pt_v, own_v, price1_v, flow_s, gen_s, dual_s, genlow_v,
     part_send, part_recv, fw_own, fw_in, d_send, d_recv, v_send, v_recv, prev_v,
-    ahead_send, ahead_recv, state_send, state_recv, far_new,
+    ahead_send, ahead_recv, state_send, state_recv,
     ar_s, ar_r, acc_v, change_v, idx_v, table_v, table_s,
     in_sem, ps_sem, pr_sem, fs_sem, fr_sem, tm_sem, ar_sem, ahead_sem, ready,
 ):
@@ -98,6 +98,8 @@
     has = tuple((p >= 0) & (p < nr) for p in place)
     peer = tuple(jnp.clip(p, 0, nr - 1) for p in place)
     count = tuple(jnp.where(h, 1, 0) for h in has)
+    is_odd = odd == 1
+    far_of = (has[FAR] & (odd == 0), has[FAR] & is_odd)
     first_window = (2 * lb * odd, 2 * lb * (1 - odd), lb)
 
     barrier = pltpu.get_barrier_semaphore()
@@ -207,9 +209,11 @@
             ahead_sem.at[0], ahead_sem.at[1 + it], "region", peer[FAR],
         )
 
-    def state_copy():
+    def state_copy(count):
+        slots = pl.ds(0, count)
         return remote(
-            state_send, state_recv, ahead_sem.at[0], ahead_sem.at[3], "region", peer[FAR]
+            state_send.at[slots], state_recv.at[slots], ahead_sem.at[0], ahead_sem.at[3],
+            "region", peer[FAR],
         )
 
     def sent(it):
@@ -218,10 +222,15 @@
             def _():
                 ref = part_send.at[it, side]
                 pltpu.make_async_copy(ref, ref, ps_sem.at[side]).wait()
-                ref = fw_own.at[it]
-                if side == FAR:
-                    ref = fw_own.at[it, pl.ds(0, nch - (known, early)[it])]
-                pltpu.make_async_copy(ref, ref, fs_sem.at[side]).wait()
+                if it == 1 or side == NEAR:
+                    ref = fw_own.at[it, pl.ds(0, nch - early if side == FAR else nch)]
+                    pltpu.make_async_copy(ref, ref, fs_sem.at[side]).wait()
+        if it == 0:
+            for parity in (0, 1):
+                @pl.when(far_of[parity])
+                def _():
+                    ref = fw_own.at[0, pl.ds(0, nch - parity * known)]
+                    pltpu.make_async_copy(ref, ref, fs_sem.at[FAR]).wait()
 
     at_near, at_own, at_gens = lines, 2 * lines, 3 * lines
 
@@ -333,8 +342,8 @@
         new = stepped(now, sp, total, caps_of(ch))
         fw_own[it, ch] = (2.0 * new - now).astype(bf16)
 
-        if ch < nch - (known, early)[it]:
-            @pl.when(has[FAR])
+        if ch < nch - (known, early)[it] or it == 0:
+            @pl.when(has[FAR] if ch < nch - (known, early)[it] else far_of[0])
             def _():
                 far_flow(it, ch).start()
 
@@ -355,33 +364,41 @@
         if it == 0:
             put_state(ahead_send.at[0, pl.ds(cols, cols + 8)], 0, nch - 1)
 
-        @pl.when(has[FAR])
-        def _():
-            if it == 1:
-                (state_copy() if early > known else ahead_copy(0)).wait_send()
-            ahead_copy(it).start()
+            @pl.when(far_of[1])
+            def _():
+                ahead_copy(0).start()
+        else:
+            for parity in (0, 1):
+                @pl.when(far_of[parity])
+                def _():
+                    slots = early - parity * known
+                    (state_copy(slots) if slots else ahead_copy(0)).wait_send()
+                    ahead_copy(1).start()
 
     def state_start():
-        for s in range(early - known):
+        for s in range(early):
             put_state(state_send.at[s], 1, nch - early + s)
-
-        @pl.when(has[FAR])
-        def _():
-            ahead_copy(0).wait_send()
-            state_copy().start()
+        for parity in (0, 1):
+            slots = early - parity * known
+            if slots:
+                @pl.when(far_of[parity])
+                def _():
+                    if parity == 1:
+                        ahead_copy(0).wait_send()
+                    state_copy(slots).start()
 
     def ahead_low(it, sp, ch):
         count = (known, early)[it]
         s = ch - (nch - count)
         total = ahead_recv[it, s * cols : (s + 1) * cols] + part_send[it, FAR, ch]
-        if it == 0 or ch >= nch - known:
-            now = far_new[...] if it == 1 else ahead_recv[0, cols : 2 * cols]
-            cap = ahead_recv[0, 2 * cols : 2 * cols + 1]
+        if it == 0:
+            now, cap = ahead_recv[0, cols : 2 * cols], ahead_recv[0, 2 * cols : 2 * cols + 1]
         else:
             now, cap = state_recv[s, :cols], state_recv[s, cols : cols + 1]
         new = stepped(now, sp, total, cap)
         if it == 0:
-            far_new[...] = new
+            state_recv[early - 1, :cols] = new
+            state_recv[early - 1, cols:] = ahead_recv[0, 2 * cols :  2 * cols + 8]
         return (2.0 * new - now).astype(bf16)
 
     def send_near(it):
@@ -408,10 +425,10 @@
             a_v[:, at_near:at_own], other, nt_dims, preferred_element_type=f32
         )
 
-    def push_far(it, sp, chunks):
+    def push_far(it, sp, chunks, ahead):
         lows = []
         for ch in chunks:
-            if ch >= nch - (known, early)[it]:
+            if ch in ahead:
                 lows.append(ahead_low(it, sp, ch))
             else:
                 far_flow(it, ch).wait_recv()
@@ -425,30 +442,43 @@
         )
 
     def push(it, sp, meanwhile, finish):
-        count = (known, early)[it]
-        more = max(nch // 2 - count, 0)
-        first = [*range(nch - count, nch), *range(more)]
-        last = [*range(more, nch - count)]
-        if it == 0 and early > known:
+        if it == 0 and early > 0:
             state_start()
         push_own(it)
         if it == 1:
             meanwhile()
-        if count > 0:
-            @pl.when(has[FAR])
-            def _():
-                ahead_copy(it).wait_recv()
-                if it == 1 and early > known:
-                    state_copy().wait_recv()
-                acc_v[...] += push_far(it, sp, first)
-
+        plans = []
+        for parity in (0, 1):
+            n = early if it == 1 else known * (1 - parity)
+            more = max(nch // 2 - n, 0)
+            plans.append(
+                ([*range(nch - n, nch)], [*range(nch - n, nch), *range(more)], [*range(more, nch - n)])
+            )
+
+        def far_first(parity):
+            ahead, first, _ = plans[parity]
+            if first:
+                @pl.when(far_of[parity])
+                def _():
+                    if ahead:
+                        ahead_copy(it).wait_recv()
+                    if it == 1 and early - (1 - parity) * known:
+                        state_copy(early - (1 - parity) * known).wait_recv()
+                    acc_v[...] += push_far(it, sp, first, ahead)
+
+        far_first(0)
+        if it == 1:
+            far_first(1)
         push_near(it)
         if it == 0:
+            far_first(1)
             meanwhile()
 
-        @pl.when(has[FAR])
-        def _():
-            finish(acc_v[...] + push_far(it, sp, last))
+        for parity in (0, 1):
+            @pl.when(far_of[parity])
+            def _():
+                ahead, _, last = plans[parity]
+                finish(acc_v[...] + push_far(it, sp, last, ahead))
 
         @pl.when(jnp.logical_not(has[FAR]))
         def _():
@@ -662,9 +692,8 @@
         V((scen, gens), f32),
         V((2, ahead_rows, cw), f32),
         V((2, ahead_rows, cw), f32),
-        V((max(early - 1, 1), cols + 8, cw), f32),
-        V((max(early - 1, 1), cols + 8, cw), f32),
-        V((cols, cw), f32),
+        V((max(early, 1), cols + 8, cw), f32),
+        V((max(early, 1), cols + 8, cw), f32),
         V((1, 128), f32),
         V((nt * nr, 1, 128), f32),
         V((buses, cols), f32),

time: 23.5 us -> 23.5 us (level)
  no operation moved by 1% of the time
where the time goes in v5:
time: 23.5 us; the launch traced here: 23.3 us
  Pallas kernels  21.4 us (91%)
  between operations  1.94 us (8%)
    pallas_call x1, Pallas kernels, shards(): pl.pallas_call(functools.partial(kernel, dims), out_shape=tuple((V(shape,...  20.5 us
    pallas_call x1, Pallas kernels, shards(): pl.pallas_call(writer, out_shape=tuple((jax.ShapeDtypeStruct(shape, f32)...  0.86 us

profile of v5, /device:TPU:1, one launch (start us, length us, event | category | flops | bytes accessed | tf_op | source)
XLA Modules:
  0.0 23.3 jit_solution(5634318443227963218)
XLA Ops:
  1.9 20.5 %shard_map.174 = (f32[128,128]{1,0:T(8,128)S(1)}, f32[512,128]{1,0:T(8,128)S(1)}, f32[512,128]{1,0:T(8,128)S(1)}, f32[128,128]{1,0:T(8,128)S(1)}) custom-call(s32[1]{0:T(128)S(6)} %copy.23.gen_bus, f32[]{:T(128)S(6)} %copy.24.weight, s32[1,32]{1,0:T(1,128)} %bitcast.24, s32[1,32]{1,0:T(1,128)} %bitcast.25, bf16[32,128,128]{2,1,0:T(8,128)(2,1)} %tiles.1, ...), custom_call_target="tpu_custom_call" | custom-call | tf_op jit(solution)/shard_map/pallas_call | solution.py:716
  22.5 0.9 %shard_map.175 = (f32[128,128]{1,0:T(8,128)}, f32[512,128]{1,0:T(8,128)}, f32[512,128]{1,0:T(8,128)}, f32[128,128]{1,0:T(8,128)}) custom-call(f32[128,128]{1,0:T(8,128)S(1)} %get-tuple-element.12.refs_0_, f32[512,128]{1,0:T(8,128)S(1)} %get-tuple-element.13.refs_1_, f32[512,128]{1,0:T(8,128)S(1)} %get-tuple-element.14.refs_2_, ...), custom_call_target="tpu_custom_call" | custom-call | tf_op jit(solution)/shard_map/pallas_call | solution.py:729

commit v6 on v5

--- a/solution.py
+++ b/solution.py
@@ -407,13 +407,33 @@
             near_flow(it).start()
 
     nt_dims = (((1,), (1,)), ((), ()))
+    push_rows = buses // 2 if bb % 2 == 0 else buses
 
     def joined(get, n):
         return jnp.concatenate([get(ch) for ch in range(n)], axis=1) if n > 1 else get(0)
 
+    rows_at = [pl.ds(at, push_rows) for at in range(0, buses, push_rows)]
+
+    def add_up(lines_of, low, use):
+        for rows in rows_at:
+            wide = [a_v[rows, at] for at in lines_of]
+            use(
+                rows,
+                lax.dot_general(
+                    jnp.concatenate(wide, axis=1) if len(wide) > 1 else wide[0], low, nt_dims,
+                    preferred_element_type=f32,
+                ),
+            )
+
+    def keep(rows, sums):
+        acc_v[rows] = sums
+
+    def accumulate(rows, sums):
+        acc_v[rows] += sums
+
     def push_own(it):
         mine = jnp.concatenate([fw_own[it, ch] for ch in range(nch)] + [genlow_v[...]], axis=1)
-        acc_v[...] = lax.dot_general(a_v[:, at_own:], mine, nt_dims, preferred_element_type=f32)
+        add_up([pl.ds(at_own, lines + gens)], mine, keep)
 
     def push_near(it):
         @pl.when(has[NEAR])
@@ -421,11 +441,9 @@
             near_flow(it).wait_recv()
 
         other = joined(lambda ch: fw_in[it, NEAR, ch], nch)
-        acc_v[...] += lax.dot_general(
-            a_v[:, at_near:at_own], other, nt_dims, preferred_element_type=f32
-        )
-
-    def push_far(it, sp, chunks, ahead):
+        add_up([pl.ds(at_near, lines)], other, accumulate)
+
+    def push_far(it, sp, chunks, ahead, use):
         lows = []
         for ch in chunks:
             if ch in ahead:
@@ -433,15 +451,12 @@
             else:
                 far_flow(it, ch).wait_recv()
                 lows.append(fw_in[it, FAR, ch])
-        wide = [a_v[:, ch * cw : (ch + 1) * cw] for ch in chunks]
-        many = len(chunks) > 1
-        return lax.dot_general(
-            jnp.concatenate(wide, axis=1) if many else wide[0],
-            jnp.concatenate(lows, axis=1) if many else lows[0],
-            nt_dims, preferred_element_type=f32,
-        )
-
-    def push(it, sp, meanwhile, finish):
+        add_up(
+            [pl.ds(ch * cw, cw) for ch in chunks],
+            jnp.concatenate(lows, axis=1) if len(lows) > 1 else lows[0], use,
+        )
+
+    def push(it, sp, meanwhile, finish, done):
         if it == 0 and early > 0:
             state_start()
         push_own(it)
@@ -464,7 +479,7 @@
                         ahead_copy(it).wait_recv()
                     if it == 1 and early - (1 - parity) * known:
                         state_copy(early - (1 - parity) * known).wait_recv()
-                    acc_v[...] += push_far(it, sp, first, ahead)
+                    push_far(it, sp, first, ahead, accumulate)
 
         far_first(0)
         if it == 1:
@@ -478,11 +493,14 @@
             @pl.when(far_of[parity])
             def _():
                 ahead, _, last = plans[parity]
-                finish(acc_v[...] + push_far(it, sp, last, ahead))
+                push_far(it, sp, last, ahead, lambda rows, sums: finish(rows, acc_v[rows] + sums))
+                done()
 
         @pl.when(jnp.logical_not(has[FAR]))
         def _():
-            finish(acc_v[...])
+            for rows in rows_at:
+                finish(rows, acc_v[rows])
+            done()
 
     def ramp_step(it, gbar, prev, sd):
         earlier = prev if cols == scen else jnp.concatenate([prev, gbar[: cols - scen]], axis=0)
@@ -564,13 +582,16 @@
         d_send[1] = dual_one[:scen]
         dual_copy(1).start()
 
-    def price_now(pushed):
-        new = price_v[...] + sd1 * (demand_v[...] - pushed)
-        price1_v[...] = new
-        dual_row = both_halves(change_v[...] + fold((new - price_v[...]) ** 2))
-        ar_s[...] = jnp.where(low, primal_row, dual_row)
-
-    push(0, sp1, ramp_now, price_now)
+    def price_now(rows, pushed):
+        old = price_v[rows]
+        new = old + sd1 * (demand_v[rows] - pushed)
+        price1_v[rows] = new
+        change_v[...] += fold((new - old) ** 2)
+
+    def rows_ready():
+        ar_s[...] = jnp.where(low, primal_row, both_halves(change_v[...]))
+
+    push(0, sp1, ramp_now, price_now, rows_ready)
 
     if n_stages > 0:
         stage_wait(n_stages - 1)
@@ -623,10 +644,10 @@
             o_flow[b * blk : (b + 1) * blk, :] = flow_s[2, :, b * blk : (b + 1) * blk].T
         o_gen[...] = gen_s[2].T
 
-    def price_out(pushed):
-        o_price[...] = price1_v[...] + sd2 * (demand_v[...] - pushed)
-
-    push(1, sp2, results, price_out)
+    def price_out(rows, pushed):
+        o_price[rows] = price1_v[rows] + sd2 * (demand_v[rows] - pushed)
+
+    push(1, sp2, results, price_out, lambda: None)
 
     dual_copy(1).wait_send()
     prev_copy(1).wait_send()

time: 23.5 us -> 23.5 us (level)
  no operation moved by 1% of the time
where the time goes in v6:
time: 23.5 us; the launch traced here: 23.3 us
  Pallas kernels  21.3 us (91%)
  between operations  1.94 us (8%)
    pallas_call x1, Pallas kernels, shards(): pl.pallas_call(functools.partial(kernel, dims), out_shape=tuple((V(shape,...  20.5 us
    pallas_call x1, Pallas kernels, shards(): pl.pallas_call(writer, out_shape=tuple((jax.ShapeDtypeStruct(shape, f32)...  0.86 us

profile of v6, /device:TPU:1, one launch (start us, length us, event | category | flops | bytes accessed | tf_op | source)
XLA Modules:
  0.0 23.3 jit_solution(16639302727722636484)
XLA Ops:
  1.9 20.5 %shard_map.174 = (f32[128,128]{1,0:T(8,128)S(1)}, f32[512,128]{1,0:T(8,128)S(1)}, f32[512,128]{1,0:T(8,128)S(1)}, f32[128,128]{1,0:T(8,128)S(1)}) custom-call(s32[1]{0:T(128)S(6)} %copy.23.gen_bus, f32[]{:T(128)S(6)} %copy.24.weight, s32[1,32]{1,0:T(1,128)} %bitcast.24, s32[1,32]{1,0:T(1,128)} %bitcast.25, bf16[32,128,128]{2,1,0:T(8,128)(2,1)} %tiles.1, ...), custom_call_target="tpu_custom_call" | custom-call | tf_op jit(solution)/shard_map/pallas_call | solution.py:737
  22.4 0.9 %shard_map.175 = (f32[128,128]{1,0:T(8,128)}, f32[512,128]{1,0:T(8,128)}, f32[512,128]{1,0:T(8,128)}, f32[128,128]{1,0:T(8,128)}) custom-call(f32[128,128]{1,0:T(8,128)S(1)} %get-tuple-element.12.refs_0_, f32[512,128]{1,0:T(8,128)S(1)} %get-tuple-element.13.refs_1_, f32[512,128]{1,0:T(8,128)S(1)} %get-tuple-element.14.refs_2_, ...), custom_call_target="tpu_custom_call" | custom-call | tf_op jit(solution)/shard_map/pallas_call | solution.py:750

commit v7 on v6

--- a/solution.py
+++ b/solution.py
@@ -60,7 +60,7 @@
 
 def partners(x, n):
     if n & (n - 1) == 0:
-        return [(m, flip(x, m)) for m in [*range(n // 2, n), *range(n // 2 - 1, 0, -1)]]
+        return [(m, flip(x, m)) for m in [n // 2, *range(n - 1, n // 2, -1), *range(n // 2 - 1, 0, -1)]]
     return [(m, lax.rem(x + m, n)) for m in range(1, n)]
 
 
@@ -595,7 +595,6 @@
 
     if n_stages > 0:
         stage_wait(n_stages - 1)
-    sent(0)
     others_t = partners(t, nt) + [(0, t)]
     others_r = partners(r, nr) + [(0, r)]
     for k, to_r in others_r:
@@ -610,6 +609,7 @@
                     device_id_type=MESH,
                 ).start()
     others = ar_r.at[pl.ds(1, nt * nr - 1)]
+    sent(0)
     set_pt(price1_v)
     for ch in range(0, nch, per_dot):
         far_sums(1, ch)
@@ -623,9 +623,10 @@
     if early > 0:
         ahead_start(1)
     pltpu.make_async_copy(others, others, ar_sem.at[1]).wait()
-    summed = ar_s[...]
-    for at in range(1, nt * nr):
-        summed = summed + ar_r[at]
+    parts = [ar_s[...]] + [ar_r[at] for at in range(1, nt * nr)]
+    while len(parts) > 1:
+        parts = [a + b for a, b in zip(parts[::2], parts[1::2])] + parts[len(parts) // 2 * 2 :]
+    summed = parts[0]
     primal_mean = jnp.sum(jnp.where(low, summed, 0.0), axis=1, keepdims=True) / count_p
     dual_mean = jnp.sum(jnp.where(low, 0.0, summed), axis=1, keepdims=True) / count_d
     w2 = jnp.sqrt(w1 * jnp.sqrt((dual_mean + tiny) / (primal_mean + tiny)))

time: 23.5 us -> 23.4 us (level)
  no operation moved by 1% of the time
where the time goes in v7:
time: 23.4 us; the launch traced here: 23.3 us
  Pallas kernels  21.3 us (91%)
  between operations  1.94 us (8%)
    pallas_call x1, Pallas kernels, shards(): pl.pallas_call(functools.partial(kernel, dims), out_shape=tuple((V(shape,...  20.5 us
    pallas_call x1, Pallas kernels, shards(): pl.pallas_call(writer, out_shape=tuple((jax.ShapeDtypeStruct(shape, f32)...  0.86 us

profile of v7, /device:TPU:1, one launch (start us, length us, event | category | flops | bytes accessed | tf_op | source)
XLA Modules:
  0.0 23.3 jit_solution(8711522917668833919)
XLA Ops:
  1.9 20.5 %shard_map.174 = (f32[128,128]{1,0:T(8,128)S(1)}, f32[512,128]{1,0:T(8,128)S(1)}, f32[512,128]{1,0:T(8,128)S(1)}, f32[128,128]{1,0:T(8,128)S(1)}) custom-call(s32[1]{0:T(128)S(6)} %copy.23.gen_bus, f32[]{:T(128)S(6)} %copy.24.weight, s32[1,32]{1,0:T(1,128)} %bitcast.24, s32[1,32]{1,0:T(1,128)} %bitcast.25, bf16[32,128,128]{2,1,0:T(8,128)(2,1)} %tiles.1, ...), custom_call_target="tpu_custom_call" | custom-call | tf_op jit(solution)/shard_map/pallas_call | solution.py:738
  22.4 0.9 %shard_map.175 = (f32[128,128]{1,0:T(8,128)}, f32[512,128]{1,0:T(8,128)}, f32[512,128]{1,0:T(8,128)}, f32[128,128]{1,0:T(8,128)}) custom-call(f32[128,128]{1,0:T(8,128)S(1)} %get-tuple-element.12.refs_0_, f32[512,128]{1,0:T(8,128)S(1)} %get-tuple-element.13.refs_1_, f32[512,128]{1,0:T(8,128)S(1)} %get-tuple-element.14.refs_2_, ...), custom_call_target="tpu_custom_call" | custom-call | tf_op jit(solution)/shard_map/pallas_call | solution.py:751

commit v8 on v7

--- a/solution.py
+++ b/solution.py
@@ -456,7 +456,7 @@
             jnp.concatenate(lows, axis=1) if len(lows) > 1 else lows[0], use,
         )
 
-    def push(it, sp, meanwhile, finish, done):
+    def push(it, sp, meanwhile, settle, finish, done):
         if it == 0 and early > 0:
             state_start()
         push_own(it)
@@ -488,18 +488,19 @@
         if it == 0:
             far_first(1)
             meanwhile()
+        settle()
 
         for parity in (0, 1):
             @pl.when(far_of[parity])
             def _():
                 ahead, _, last = plans[parity]
-                push_far(it, sp, last, ahead, lambda rows, sums: finish(rows, acc_v[rows] + sums))
+                push_far(it, sp, last, ahead, finish)
                 done()
 
         @pl.when(jnp.logical_not(has[FAR]))
         def _():
             for rows in rows_at:
-                finish(rows, acc_v[rows])
+                finish(rows, None)
             done()
 
     def ramp_step(it, gbar, prev, sd):
@@ -584,14 +585,14 @@
 
     def price_now(rows, pushed):
         old = price_v[rows]
-        new = old + sd1 * (demand_v[rows] - pushed)
+        new = old + sd1 * (demand_v[rows] - (acc_v[rows] if pushed is None else acc_v[rows] + pushed))
         price1_v[rows] = new
         change_v[...] += fold((new - old) ** 2)
 
     def rows_ready():
         ar_s[...] = jnp.where(low, primal_row, both_halves(change_v[...]))
 
-    push(0, sp1, ramp_now, price_now, rows_ready)
+    push(0, sp1, ramp_now, lambda: None, price_now, rows_ready)
 
     if n_stages > 0:
         stage_wait(n_stages - 1)
@@ -645,10 +646,13 @@
             o_flow[b * blk : (b + 1) * blk, :] = flow_s[2, :, b * blk : (b + 1) * blk].T
         o_gen[...] = gen_s[2].T
 
+    def price_but_last():
+        acc_v[...] = price1_v[...] + sd2 * (demand_v[...] - acc_v[...])
+
     def price_out(rows, pushed):
-        o_price[rows] = price1_v[rows] + sd2 * (demand_v[rows] - pushed)
-
-    push(1, sp2, results, price_out, lambda: None)
+        o_price[rows] = acc_v[rows] if pushed is None else acc_v[rows] - sd2 * pushed
+
+    push(1, sp2, results, price_but_last, price_out, lambda: None)
 
     dual_copy(1).wait_send()
     prev_copy(1).wait_send()

time: 23.4 us -> 23.4 us (level)
  no operation moved by 1% of the time
where the time goes in v8:
time: 23.4 us; the launch traced here: 23.3 us
  Pallas kernels  21.3 us (91%)
  between operations  1.94 us (8%)
    pallas_call x1, Pallas kernels, shards(): pl.pallas_call(functools.partial(kernel, dims), out_shape=tuple((V(shape,...  20.5 us
    pallas_call x1, Pallas kernels, shards(): pl.pallas_call(writer, out_shape=tuple((jax.ShapeDtypeStruct(shape, f32)...  0.86 us

profile of v8, /device:TPU:1, one launch (start us, length us, event | category | flops | bytes accessed | tf_op | source)
XLA Modules:
  0.0 23.3 jit_solution(8385242426033759889)
XLA Ops:
  1.9 20.5 %shard_map.174 = (f32[128,128]{1,0:T(8,128)S(1)}, f32[512,128]{1,0:T(8,128)S(1)}, f32[512,128]{1,0:T(8,128)S(1)}, f32[128,128]{1,0:T(8,128)S(1)}) custom-call(s32[1]{0:T(128)S(6)} %copy.23.gen_bus, f32[]{:T(128)S(6)} %copy.24.weight, s32[1,32]{1,0:T(1,128)} %bitcast.24, s32[1,32]{1,0:T(1,128)} %bitcast.25, bf16[32,128,128]{2,1,0:T(8,128)(2,1)} %tiles.1, ...), custom_call_target="tpu_custom_call" | custom-call | tf_op jit(solution)/shard_map/pallas_call | solution.py:742
  22.4 0.9 %shard_map.175 = (f32[128,128]{1,0:T(8,128)}, f32[512,128]{1,0:T(8,128)}, f32[512,128]{1,0:T(8,128)}, f32[128,128]{1,0:T(8,128)}) custom-call(f32[128,128]{1,0:T(8,128)S(1)} %get-tuple-element.12.refs_0_, f32[512,128]{1,0:T(8,128)S(1)} %get-tuple-element.13.refs_1_, f32[512,128]{1,0:T(8,128)S(1)} %get-tuple-element.14.refs_2_, ...), custom_call_target="tpu_custom_call" | custom-call | tf_op jit(solution)/shard_map/pallas_call | solution.py:755
